TPU v7x, 128 devices: a whole 4x4x4 slice. The times are simulated.
128 devices in a mesh: dom: 128 (over y, x, z, core).
Axes of the slice: x: 4, y: 4, z: 4, core: 2. Of those that a mesh axis runs over, the one named last changes fastest.
Arguments:
- velocity: bfloat16 [3, 512, 65536], P(None, None, 'dom'), may hold values from -1.1953125 to 1.1953125
- inverse_sizes: float32 [3, 65536], P(None, 'dom'), may hold values from 0.5 to 2
- resample_x: float32 [2, 8, 8, 65536], P(None, None, None, 'dom'), may hold values from 0 to 0.25
- resample_y: float32 [2, 4, 8, 65536], P(None, None, None, 'dom'), may hold values from 0 to 0.25
- resample_z: float32 [2, 4, 8, 65536], P(None, None, None, 'dom'), may hold values from 0 to 0.25
- piece_target: int32 [2, 65536], P(None, 'dom'), may hold values from 0 to 511, as said below
- target_brick: int32 [65536, 1], P('dom'), may hold values from 0 to 127; in each aligned block of 512 rows (0 to 511, 512 to 1023, ...) at most 16 rows name the same one
- target_block: int32 [65536], P('dom'), may hold values from 0 to 2047
- brick_home: int32 [128], replicated, may hold values from 0 to 127, each once
Outputs:
- bricks: float32 [128, 2048, 128], P('dom')
Inputs may be any that keep to these rules, and one draw needn't show every extreme that they name: `piece_target`: among the 2 x 512 entries of one device's columns every value appears exactly twice. `target_brick`: in the rows of one device no brick is named more than 16 times, and in some device's rows some brick is named exactly 16 times. `brick_home`: every device is the home of exactly one brick.
All inputs are finite; a program needn't handle non-finite values.
Results may differ from a plain program's by a relative error of at most 0.0023.
Values sent between devices are 32-bit elements; how exact they have to be, the bound alone decides.
A program may use at most 192 MiB of HBM per device.

v0:
```python
import math

import jax
import jax.numpy as jnp
import numpy as np
from jax import lax
from jax.sharding import PartitionSpec as P

EYN = 8
EZN = 16
BLOCKS = 2048


GLL_NODES = [
    -1.0,
    -0.8717401485096066,
    -0.5917001814331423,
    -0.2092992179024789,
    0.2092992179024789,
    0.5917001814331423,
    0.8717401485096066,
    1.0,
]


def extended(cells, sides, width):
    for axis, dim in sides:
        count = lax.axis_size(axis)
        head = lax.slice_in_dim(cells, 0, width, axis=dim)
        tail = lax.slice_in_dim(cells, cells.shape[dim] - width, cells.shape[dim], axis=dim)
        cells = jnp.concatenate(
            [
                lax.ppermute(tail, axis, [(i, (i + 1) % count) for i in range(count)]),
                cells,
                lax.ppermute(head, axis, [((i + 1) % count, i) for i in range(count)]),
            ],
            axis=dim,
        )
    return cells


def derivative_operator():
    barycentric = []
    for first in range(8):
        product_term = 1.0
        for other in range(8):
            if other != first:
                product_term = product_term * (GLL_NODES[first] - GLL_NODES[other])
        barycentric.append(1.0 / product_term)
    matrix_rows = []
    for first in range(8):
        row_values = []
        for second in range(8):
            if second == first:
                row_values.append(0.0)
            else:
                row_values.append(
                    barycentric[second]
                    / barycentric[first]
                    / (GLL_NODES[first] - GLL_NODES[second])
                )
        row_values[first] = -sum(row_values)
        matrix_rows.append(row_values)
    diff_matrix = np.array(matrix_rows)
    identity = np.eye(8)
    return np.concatenate(
        [
            np.kron(np.kron(diff_matrix, identity), identity),
            np.kron(np.kron(identity, diff_matrix), identity),
            np.kron(np.kron(identity, identity), diff_matrix),
        ],
        axis=0,
    )


def stitch_stream(gradient, from_prev, from_next):
    low_face = gradient[:, 0]
    high_face = gradient[:, 7]
    from_below = jnp.concatenate([from_prev[:, :, None, :], high_face[:, :, :-1, :]], axis=2)
    from_above = jnp.concatenate([low_face[:, :, 1:, :], from_next[:, :, None, :]], axis=2)
    return gradient.at[:, 0].set(low_face + from_below).at[:, 7].set(high_face + from_above)


def stitch_cross(gradient):
    cross_count = gradient.shape[-1]
    column = jnp.arange(cross_count, dtype=jnp.int32)
    normal = column // EZN
    spanwise = column % EZN
    low_face = gradient[:, :, 0]
    high_face = gradient[:, :, 7]
    from_below = jnp.where(normal > 0, jnp.roll(high_face, EZN, axis=-1), 0.0)
    from_above = jnp.where(normal < EYN - 1, jnp.roll(low_face, -EZN, axis=-1), 0.0)
    gradient = (
        gradient.at[:, :, 0].set(low_face + from_below).at[:, :, 7].set(high_face + from_above)
    )
    low_face = gradient[:, :, :, 0]
    high_face = gradient[:, :, :, 7]
    from_before = jnp.where(
        spanwise == 0, jnp.roll(high_face, 1 - EZN, axis=-1), jnp.roll(high_face, 1, axis=-1)
    )
    from_after = jnp.where(
        spanwise == EZN - 1, jnp.roll(low_face, EZN - 1, axis=-1), jnp.roll(low_face, -1, axis=-1)
    )
    gradient = (
        gradient.at[:, :, :, 0]
        .set(low_face + from_before)
        .at[:, :, :, 7]
        .set(high_face + from_after)
    )
    points = jnp.arange(8, dtype=jnp.int32)
    on_face = (points == 0) | (points == 7)
    at_wall = (points[:, None] == 0) & (normal[None, :] == 0) | (points[:, None] == 7) & (
        normal[None, :] == EYN - 1
    )
    edge_factor = jnp.where(on_face, 0.5, 1.0).astype(jnp.float32)
    normal_factor = jnp.where(on_face[:, None] & jnp.logical_not(at_wall), 0.5, 1.0).astype(
        jnp.float32
    )
    factors = (
        edge_factor[:, None, None, None, None]
        * normal_factor[None, :, None, None, :]
        * edge_factor[None, None, :, None, None]
    )
    return gradient * factors[None]


def middle_eigen(gradient):
    strain = [
        [0.5 * (gradient[first][second] + gradient[second][first]) for second in range(3)]
        for first in range(3)
    ]
    rotation = [
        [0.5 * (gradient[first][second] - gradient[second][first]) for second in range(3)]
        for first in range(3)
    ]
    moment = [
        [
            sum(
                (
                    strain[first][inner] * strain[inner][second]
                    + rotation[first][inner] * rotation[inner][second]
                    for inner in range(3)
                )
            )
            for second in range(3)
        ]
        for first in range(3)
    ]
    mean_diag = (moment[0][0] + moment[1][1] + moment[2][2]) / 3.0
    shift_x = moment[0][0] - mean_diag
    shift_y = moment[1][1] - mean_diag
    shift_z = moment[2][2] - mean_diag
    offdiag = (
        moment[0][1] * moment[0][1] + moment[0][2] * moment[0][2] + moment[1][2] * moment[1][2]
    )
    spread = (shift_x * shift_x + shift_y * shift_y + shift_z * shift_z + 2.0 * offdiag) / 6.0
    determinant = (
        shift_x * (shift_y * shift_z - moment[1][2] * moment[1][2])
        - moment[0][1] * (moment[0][1] * shift_z - moment[1][2] * moment[0][2])
        + moment[0][2] * (moment[0][1] * moment[1][2] - shift_y * moment[0][2])
    )
    halfdet = 0.5 * determinant
    discrim = jnp.maximum(spread * spread * spread - halfdet * halfdet, 0.0)
    angles = jnp.arctan2(jnp.sqrt(discrim), halfdet) / 3.0
    radius = 2.0 * jnp.sqrt(spread)
    largest = mean_diag + radius * jnp.cos(angles)
    smallest = mean_diag + radius * jnp.cos(angles + 2.0 * math.pi / 3.0)
    return 3.0 * mean_diag - largest - smallest


def resample(lambda_two, weight_x, weight_y, weight_z):
    highest = lax.Precision.HIGHEST
    along_x = jnp.einsum("oaie,ijke->oajke", weight_x, lambda_two, precision=highest)
    along_y = jnp.einsum("obje,oajke->oabke", weight_y, along_x, precision=highest)
    along_z = jnp.einsum("ocke,oabke->oabce", weight_z, along_y, precision=highest)
    columns = lambda_two.shape[-1]
    return jnp.transpose(along_z.reshape(2, 128, columns), (0, 2, 1))


def pack_rows(values, owners, blocks, devices, slot_count):
    onehot = (owners[:, None] == jnp.arange(devices, dtype=jnp.int32)[None, :]).astype(jnp.int32)
    ordinal = jnp.sum((jnp.cumsum(onehot, axis=0) - 1) * onehot, axis=1)
    sendbuf = jnp.zeros((devices, slot_count, 128), jnp.float32).at[owners, ordinal].set(values)
    indices = jnp.zeros((devices, slot_count), jnp.int32).at[owners, ordinal].set(blocks)
    return (sendbuf, indices)


def shards(
    velocity,
    inverse_sizes,
    resample_x,
    resample_y,
    resample_z,
    piece_target,
    target_brick,
    target_block,
    brick_home,
):
    elements = velocity.shape[2]
    cross_count = EYN * EZN
    layers = elements // cross_count
    operator = jnp.asarray(derivative_operator(), jnp.float32).astype(jnp.bfloat16)
    products = jnp.einsum("pq,cqe->cpe", operator, velocity, preferred_element_type=jnp.float32)
    gradient = (products.reshape(3, 3, 512, elements) * inverse_sizes[None, :, None, :]).reshape(
        9, 8, 64, layers, cross_count
    )
    rim_faces = jnp.stack([gradient[:, 0, :, 0, :], gradient[:, 7, :, layers - 1, :]], axis=2)
    padded = extended(rim_faces, (("dom", 2),), 1)
    from_prev = padded[:, :, 0, :]
    from_next = padded[:, :, 3, :]
    gradient = stitch_stream(gradient, from_prev, from_next)
    gradient = stitch_cross(gradient.reshape(9, 8, 8, 8, layers, cross_count))
    lambda_two = middle_eigen(gradient.reshape(3, 3, 512, elements))
    pieces = resample(
        lambda_two.reshape(8, 8, 8, elements), resample_x, resample_y, resample_z
    ).reshape(-1, 128)
    devices = lax.axis_size("dom")
    capacity = max(2, 4 * elements // devices)
    local_ids = piece_target.reshape(-1)
    owners = brick_home[target_brick[local_ids, 0]]
    sendbuf, indices = pack_rows(pieces, owners, target_block[local_ids], devices, 2 * capacity)
    received, received_blocks = (
        lax.all_to_all(sendbuf, "dom", split_axis=0, concat_axis=0, tiled=True),
        lax.all_to_all(indices, "dom", split_axis=0, concat_axis=0, tiled=True),
    )
    brick_image = (
        jnp.zeros((BLOCKS, 128), jnp.float32)
        .at[received_blocks.reshape(-1)]
        .add(received.reshape(-1, 128))
    )
    return brick_image[None]


def solution(mesh):
    return jax.shard_map(
        shards,
        mesh=mesh,
        in_specs=(
            P(None, None, "dom"),
            P(None, "dom"),
            P(None, None, None, "dom"),
            P(None, None, None, "dom"),
            P(None, None, None, "dom"),
            P(None, "dom"),
            P("dom", None),
            P("dom"),
            P(),
        ),
        out_specs=P("dom", None, None),
        check_vma=False,
    )
```

profile of v0, /device:TPU:1, one launch (start us, length us, event | category | flops | bytes accessed | tf_op | source)
XLA Modules:
  0.0 723.6 jit_solution(10783682871805010770)
XLA Ops:
  1.4 6.5 convolution_bitcast_fusion.2
  7.9 11.9 %reshape.765 = f32[9,8,64,4,128]{4,3,2,1,0:T(4,128)} reshape(f32[3,1536,512]{2,1,0:T(8,128)} %convolution_bitcast_fusion.2) | data formatting | bytes 18874368 | tf_op jit(solution)/shard_map/reshape | solution.py:204
  19.8 5.1 copy_multiply_fusion
  25.8 3.0 collective-permute-start
  28.8 6.5 gather_fusion
  36.0 6.6 gather_fusion.1
  43.8 6.9 gather_fusion.2
  50.7 4.3 scatter_custom_fusion.1
  55.7 12.1 %all-to-all-start = ((s32[128,1,32]{2,1,0:T(1,128)}), s32[128,1,32]{2,1,0:T(1,128)S(1)}, u32[]{:S(2)}, u32[]{:S(2)}) async-start(s32[128,1,32]{2,1,0:T(1,128)} %copy.114), calls=%async_computation | async-start | bytes 131072 | tf_op jit(solution)/shard_map/all_to_all | solution.py:224
  71.7 4.5 copy.148
  79.6 2.8 fusion.6
  82.4 4.7 copy.119
  87.6 3.3 copy-done.7
  91.2 3.7 copy.180
  104.7 2.9 copy.130
  109.6 6.7 fusion.5
  121.3 2.9 copy.126
  126.8 4.1 fusion.13
  130.9 30.6 %scatter.49 = f32[9,8,8,8,4,128]{5,3,2,4,1,0:T(8,128)} dynamic-update-slice(f32[9,8,8,8,4,128]{5,3,2,4,1,0:T(8,128)} %copy-done.6, f32[9,8,8,1,4,128]{5,3,2,4,1,0:T(1,128)} %bitcast.236, s32[]{:T(128)} %constant.226.clone.1, s32[]{:T(128)} %constant.226.clone.1, s32[]{:T(128)} %constant.226.clone.1, s32[]{:T(128)} %constant.226.clone.1, s32[]{:T(128)} %constant.226.clone.1, s32[]{:T(128)} %constant.226.clone.1) | dynamic-update-slice | bytes 2359300 | tf_op jit(solution)/shard_map/scatter | solution.py:106
  161.6 30.5 %scatter.50 = f32[9,8,8,8,4,128]{5,3,2,4,1,0:T(8,128)} dynamic-update-slice(f32[9,8,8,8,4,128]{5,3,2,4,1,0:T(8,128)} %scatter.49, f32[9,8,8,1,4,128]{5,3,2,4,1,0:T(1,128)S(1)} %get-tuple-element.92, s32[]{:T(128)} %constant.226.clone.1, s32[]{:T(128)} %constant.226.clone.1, s32[]{:T(128)} %constant.226.clone.1, s32[]{:T(128)} %constant.232.clone.1, s32[]{:T(128)} %constant.226.clone.1, ...) | dynamic-update-slice | bytes 2359300 | tf_op jit(solution)/shard_map/scatter | solution.py:108
  192.1 4.9 broadcast_multiply_fusion
  202.6 10.3 %subtract_bitcast_fusion = f32[8,8,8,512,1]{3,2,1,0,4:T(8,128)S(1)} fusion(f32[1,8,8,8,4,128]{5,3,2,4,1,0:T(8,128)S(1)} %get-tuple-element.89, f32[1,8,8,8,4,128]{5,3,2,4,1,0:T(8,128)S(1)} %get-tuple-element.91, f32[1,8,8,8,4,128]{5,3,2,4,1,0:T(8,128)S(1)} %get-tuple-element.88, f32[1,8,8,8,4,128]{5,3,2,4,1,0:T(8,128)S(1)} %get-tuple-element.90, ...), kind=kLoop, calls=%fused_computation.80 | loop fusion | flops 12320768 | bytes 7340032 | tf_op jit(solution)/shard_map/sub | solution.py:168
  212.9 13.5 %copy.147 = f32[8,8,8,512,1]{0,2,4,1,3:T(8,128)} copy(f32[8,8,8,512,1]{3,2,1,0,4:T(8,128)S(1)} %subtract_bitcast_fusion) | data formatting | bytes 2097152 | tf_op jit(solution)/shard_map/sub | solution.py:168
  226.4 80.9 %convolution_bitcast_fusion = f32[2,8,8,8,512]{1,3,0,2,4:T(8,128)} fusion(f32[8,8,8,512,1]{0,2,4,1,3:T(8,128)} %copy.147, f32[2,8,8,512,1]{2,1,0,4,3:T(8,128)} %copy.148), kind=kOutput, calls=%fused_computation.8 | convolution fusion | flops 50331648 | bytes 3407872 | tf_op jit(solution)/shard_map/oaie,ijke->oajke/dot_general | solution.py:173
  307.3 33.1 %copy.141 = f32[2,8,8,8,512]{3,2,1,4,0:T(8,128)} copy(f32[2,8,8,8,512]{1,3,0,2,4:T(8,128)} %convolution_bitcast_fusion) | data formatting | bytes 4194304 | tf_op jit(solution)/shard_map/oaie,ijke->oajke/transpose | solution.py:173
  340.4 34.0 %convolution_bitcast_fusion.1 = f32[2,8,4,8,512]{3,2,1,4,0:T(4,128)} fusion(f32[2,8,8,8,512]{3,2,1,4,0:T(8,128)} %copy.141, f32[2,4,8,512,1]{2,1,4,3,0:T(4,128)} %copy.149), kind=kOutput, calls=%fused_computation.9 | convolution fusion | flops 25165824 | bytes 3276800 | tf_op jit(solution)/shard_map/obje,oajke->oabke/dot_general | solution.py:174
  374.4 272.6 %fusion.2 = f32[2,8,4,4,512]{1,3,2,4,0:T(4,128)} fusion(f32[2,4,8,512,1]{2,1,4,3,0:T(4,128)S(1)} %copy-done.8, f32[2,8,4,8,512]{3,2,1,4,0:T(4,128)} %convolution_bitcast_fusion.1), kind=kOutput, calls=%fused_computation.13 | convolution fusion | flops 12582912 | bytes 1703936 | tf_op jit(solution)/shard_map/ocke,oabke->oabce/dot_general | solution.py:175
  647.0 6.9 copy.145
  654.1 4.5 scatter_custom_fusion.2
  658.6 10.2 %all-to-all-start.1 = ((f32[128,32,128]{2,1,0:T(8,128)}), f32[128,32,128]{2,1,0:T(8,128)}, u32[]{:S(2)}, u32[]{:S(2)}) async-start(f32[128,32,128]{2,1,0:T(8,128)} %bitcast.234), calls=%async_computation.1 | async-start | bytes 4194304 | tf_op jit(solution)/shard_map/all_to_all | solution.py:223
  670.3 28.3 %all-to-all-done.1 = f32[128,32,128]{2,1,0:T(8,128)} async-done(((f32[128,32,128]{2,1,0:T(8,128)}), f32[128,32,128]{2,1,0:T(8,128)}, u32[]{:S(2)}, u32[]{:S(2)}) %all-to-all-start.1) | async-done | bytes 2097184 | tf_op jit(solution)/shard_map/all_to_all | solution.py:223
  698.6 24.7 %scatter_custom_fusion = f32[2048,128]{1,0:T(8,128)} fusion(s32[4096]{0:T(1024)S(1)} %bitcast.253, f32[4096,128]{1,0:T(8,128)} %bitcast.64, f32[]{:T(128)} %constant.225.clone.1), kind=kCustom, calls=%fused_computation.108 | custom fusion | flops 524288 | bytes 1049088 | tf_op jit(solution)/shard_map/scatter-add | solution.py:229
  (105 shorter events, 39.5 us)
Async XLA Ops:
  0.0 1.4 copy-start
  7.9 11.9 %copy-start.13 = (f32[3,512]{1,0:T(4,128)S(1)}, f32[3,512]{1,0:T(4,128)}, u32[]{:S(2)}) copy-start(f32[3,512]{1,0:T(4,128)} %param.23) | copy-start | bytes 18436
  24.9 3.9 copy-start.5
  24.9 3.9 copy-start.14
  24.9 3.9 copy-start.3
  25.8 53.8 %collective-permute-start = (f32[9,64,1,128]{3,1,0,2:T(8,128)}, f32[9,64,1,128]{3,1,0,2:T(8,128)S(1)}, u32[]{:S(2)}, u32[]{:S(2)}) collective-permute-start(f32[9,64,1,128]{3,1,0,2:T(8,128)} %get-tuple-element.100), channel_id=1, source_target_pairs={{0,1},{1,2},{2,3},{3,4},{4,5},{5,6},{6,7},{7,8},{8,9},{9,10},{10,1... | collective-permute-start | bytes 884744 | tf_op jit(solution)/shard_map/ppermute | solution.py:33
  28.8 58.2 %collective-permute-start.1 = (f32[9,64,1,128]{3,1,0,2:T(8,128)}, f32[9,64,1,128]{3,1,0,2:T(8,128)S(1)}, u32[]{:S(2)}, u32[]{:S(2)}) collective-permute-start(f32[9,64,1,128]{3,1,0,2:T(8,128)} %get-tuple-element.99), channel_id=1, source_target_pairs={{1,0},{2,1},{3,2},{4,3},{5,4},{6,5},{7,6},{8,7},{9,8},{10,9},{11,1... | collective-permute-start | bytes 884744 | tf_op jit(solution)/shard_map/ppermute | solution.py:35
  35.3 0.7 copy-start.2
  42.9 0.7 copy-start.18
  42.9 0.7 copy-start.16
  42.9 0.7 copy-start.17
  42.9 0.8 copy-start.4
  55.7 602.9 %all-to-all-start = ((s32[128,1,32]{2,1,0:T(1,128)}), s32[128,1,32]{2,1,0:T(1,128)S(1)}, u32[]{:S(2)}, u32[]{:S(2)}) async-start(s32[128,1,32]{2,1,0:T(1,128)} %copy.114), calls=%async_computation | async-start | bytes 131072 | tf_op jit(solution)/shard_map/all_to_all | solution.py:224
  71.7 4.5 copy-start.11
  76.2 1.7 copy-start.12
  87.2 3.7 copy-start.7
  97.6 4.0 copy-start.6
  107.6 1.8 copy-start.9
  107.6 2.0 copy-start.10
  107.6 2.0 copy-start.15
  340.4 34.0 %copy-start.8 = (f32[2,4,8,512,1]{2,1,4,3,0:T(4,128)S(1)}, f32[2,4,8,512,1]{2,1,4,3,0:T(4,128)}, u32[]{:S(2)}) copy-start(f32[2,4,8,512,1]{2,1,4,3,0:T(4,128)} %copy.150) | copy-start | bytes 393220
  658.6 40.0 %all-to-all-start.1 = ((f32[128,32,128]{2,1,0:T(8,128)}), f32[128,32,128]{2,1,0:T(8,128)}, u32[]{:S(2)}, u32[]{:S(2)}) async-start(f32[128,32,128]{2,1,0:T(8,128)} %bitcast.234), calls=%async_computation.1 | async-start | bytes 4194304 | tf_op jit(solution)/shard_map/all_to_all | solution.py:223
  668.9 54.4 %copy-start.1 = (bf16[3,512,512]{2,1,0:T(8,128)(2,1)S(1)}, bf16[3,512,512]{2,1,0:T(8,128)(2,1)}, u32[]{:S(2)}) copy-start(bf16[3,512,512]{2,1,0:T(8,128)(2,1)} %param.22) | copy-start | bytes 4718596
where the time goes:
time: 734 us; the launch traced here: 724 us
  matrix products  394 us (54%)
  local copies, waits for them, and re-layouts  204 us (28%)
  other arithmetic  70.8 us (10%)
  waiting for transfers between devices  28.3 us (4%)
  starting transfers between devices  25.3 us (3%)
    dot_general x1, matrix products, resample(): jnp.einsum('ocke,oabke->oabce', weight_z, along_y, precision=highest)  273 us
    dot_general x1, matrix products, resample(): jnp.einsum('oaie,ijke->oajke', weight_x, lambda_two, precision=highest)  80.9 us
    scatter x2, local copies, waits for them, and re-layouts, stitch_cross(): gradient = gradient.at[:, :, :, 0].set(low_face + from_before).at[:, :, :...  61.2 us
    dot_general x1, matrix products, resample(): jnp.einsum('obje,oajke->oabke', weight_y, along_x, precision=highest)  34 us
    transpose x1, local copies, waits for them, and re-layouts, resample(): jnp.einsum('oaie,ijke->oajke', weight_x, lambda_two, precision=highest)  33.1 us
    all_to_all x1, waiting for transfers between devices, shards(): lax.all_to_all(sendbuf, 'dom', split_axis=0, concat_axis=0, tiled=True)  28.3 us
    unnamed x45, local copies, waits for them, and re-layouts  26.8 us
    scatter-add x1, other arithmetic, shards(): brick_image = jnp.zeros((BLOCKS, 128), jnp.float32).at[received_blocks.re...  24.7 us
  transfers between devices with their start and end apart: 4, of which 1 were waited for; matrix products, arithmetic and copies ran while one was open for 85% of the time, Pallas kernels for 0%

commit v1 on v0

v1 whole, which is shorter than its diff:
```python
import functools

import jax
import jax.numpy as jnp
import numpy as np
from jax import lax
from jax.experimental import pallas as pl
from jax.experimental.pallas import tpu as pltpu
from jax.sharding import PartitionSpec as P

EYN = 8
EZN = 16
BLOCKS = 2048
CROSS = 128
LAYERS = 4
SLOTS = 16
BF = jnp.bfloat16
F32 = jnp.float32
I32 = jnp.int32

GLL_NODES = [
    -1.0,
    -0.8717401485096066,
    -0.5917001814331423,
    -0.2092992179024789,
    0.2092992179024789,
    0.5917001814331423,
    0.8717401485096066,
    1.0,
]

SINE_POLY = (
    0.6666666865348816,
    -0.2716042101383209,
    0.18378925323486328,
    -0.1428457647562027,
    0.11690858751535416,
    -0.09370578080415726,
    0.06620869785547256,
    -0.03593844175338745,
    0.012577426619827747,
    -0.002056414494290948,
)


def diff_matrix():
    nodes = GLL_NODES
    weights = []
    for first in range(8):
        product_term = 1.0
        for other in range(8):
            if other != first:
                product_term = product_term * (nodes[first] - nodes[other])
        weights.append(1.0 / product_term)
    rows = []
    for first in range(8):
        row = []
        for second in range(8):
            if second == first:
                row.append(0.0)
            else:
                row.append(weights[second] / weights[first] / (nodes[first] - nodes[second]))
        row[first] = -sum(row)
        rows.append(row)
    return np.array(rows)


def iota(shape, dim):
    return lax.broadcasted_iota(I32, shape, dim)


def onehot(mask):
    return jnp.where(mask, 1.0, 0.0).astype(BF)


def dot(a, b):
    return jnp.dot(a, b, preferred_element_type=F32)


def dot_nt(a, b):
    return lax.dot_general(a, b, (((1,), (1,)), ((), ())), preferred_element_type=F32)


def prep_kernel(
    vel, opface, inv, target_of, brick_of, block_of, home_of,
    low, high, low_rim, high_rim, slots, block_rows,
):
    for layer in range(LAYERS):
        lanes = slice(CROSS * layer, CROSS * layer + CROSS)
        columns = jnp.concatenate([vel[c, :, lanes] for c in range(3)], axis=1)
        faces = dot(opface[...], columns)
        for c in range(3):
            for a in range(3):
                size = inv[a : a + 1, lanes]
                low_face = faces[64 * a : 64 * a + 64, CROSS * c : CROSS * c + CROSS] * size
                high_face = faces[192 + 64 * a : 256 + 64 * a, CROSS * c : CROSS * c + CROSS] * size
                if layer == 0:
                    low_rim[3 * c + a] = low_face
                else:
                    low[layer - 1, 3 * c + a] = low_face
                if layer == LAYERS - 1:
                    high_rim[3 * c + a] = high_face
                else:
                    high[layer, 3 * c + a] = high_face

    me = lax.axis_index("dom")
    brick_row = brick_of[...]
    same = iota((128, 512), 0) == brick_row
    member = onehot(same)
    earlier = onehot(iota((512, 512), 0) < iota((512, 512), 1))
    ordinal = jnp.sum(jnp.where(same, dot(member, earlier), 0.0), axis=0, keepdims=True)
    homes = jnp.broadcast_to(home_of[...].astype(F32), (8, 128)).astype(BF)
    home = dot(homes, member)[0:1]
    row = iota((8, 512), 0)
    pair = jnp.where(row == 0, home, jnp.where(row == 1, ordinal, 0.0)).astype(BF)
    for o in range(2):
        chosen = onehot(iota((512, 512), 0) == target_of[o : o + 1, :])
        picked = dot(pair, chosen)
        slots[o : o + 1, :] = (picked[0:1] * SLOTS + picked[1:2]).astype(I32)
    to_home = onehot(iota((128, 512), 0) == home.astype(I32))
    lane = ordinal.astype(I32) + SLOTS * lax.rem(me, 8)
    at_lane = iota((128, 512), 0) == lane
    block = block_of[...]
    upper = jnp.where(at_lane, (block // 16).astype(F32), 0.0).astype(BF)
    lower = jnp.where(at_lane, (block % 16).astype(F32), 0.0).astype(BF)
    block_rows[...] = dot_nt(to_home, upper) * 16.0 + dot_nt(to_home, lower)


def middle_eigen(j00, j01, j02, j10, j11, j12, j20, j21, j22):
    p01 = j01 * j10
    p02 = j02 * j20
    p12 = j12 * j21
    m00 = j00 * j00 + p01 + p02
    m11 = j11 * j11 + p01 + p12
    m22 = j22 * j22 + p02 + p12
    m01 = 0.5 * ((j00 + j11) * (j01 + j10) + j02 * j21 + j12 * j20)
    m02 = 0.5 * ((j00 + j22) * (j02 + j20) + j01 * j12 + j21 * j10)
    m12 = 0.5 * ((j11 + j22) * (j12 + j21) + j10 * j02 + j20 * j01)
    q = (m00 + m11 + m22) * (1.0 / 3.0)
    a00 = m00 - q
    a11 = m11 - q
    a22 = m22 - q
    s01 = m01 * m01
    s02 = m02 * m02
    s12 = m12 * m12
    s = (a00 * a00 + a11 * a11 + a22 * a22) * (1.0 / 6.0) + (s01 + s02 + s12) * (1.0 / 3.0)
    det = a00 * (a11 * a22 - s12) - a11 * s02 - a22 * s01 + 2.0 * (m01 * m02 * m12)
    h = 0.5 * det
    root = jnp.sqrt(s)
    disc = jnp.maximum(s * s * s - h * h, 0.0)
    z = h / jnp.maximum(s * root + jnp.sqrt(disc), 1e-37)
    w = z * z
    poly = SINE_POLY[-1]
    for coefficient in SINE_POLY[-2::-1]:
        poly = poly * w + coefficient
    return q - 2.0 * root * (z * poly)


def slab_layers(
    layers, vel, opx, opy, opz, inv, res_x, res_y, res_z, prevs, nexts, out_rows, out_lanes,
    grad, lam, stage_z, stage_y,
):
    columns = jnp.concatenate([v[c] for c in range(3) for v in vel], axis=1)
    count = len(layers)
    for a in range(3):
        for half in range(2):
            rows = slice(256 * half, 256 * half + 256)
            if a == 0:
                part = dot(opx[rows, :], columns)
            else:
                part = dot((opy if a == 1 else opz)[...], columns[rows, :])
            for c in range(3):
                for n, layer in enumerate(layers):
                    size = inv[a : a + 1, CROSS * layer : CROSS * layer + CROSS]
                    at = CROSS * (c * count + n)
                    grad[n, 3 * c + a, rows, :] = part[:, at : at + CROSS] * size
    for n in range(count):
        for m in range(9):
            grad[n, m, 0:64, :] = 0.5 * (grad[n, m, 0:64, :] + prevs[n][m])
            grad[n, m, 448:512, :] = 0.5 * (grad[n, m, 448:512, :] + nexts[n][m])

    lane = iota((8, CROSS), 1)
    normal = lane // EZN
    span = lane % EZN

    for n in range(count):

        def plane(i, carry, n=n):
            base = pl.multiple_of(i * 64, 64)
            for m in range(9):
                view = grad.at[n, m]
                first = view[pl.ds(base, 8), :]
                last = view[pl.ds(base + 56, 8), :]
                view[pl.ds(base, 8), :] = jnp.where(
                    normal > 0, 0.5 * (first + pltpu.roll(last, EZN, 1)), first
                )
                view[pl.ds(base + 56, 8), :] = jnp.where(
                    normal < EYN - 1, 0.5 * (last + pltpu.roll(first, CROSS - EZN, 1)), last
                )
                first = view[pl.ds(base, 8, stride=8), :]
                last = view[pl.ds(base + 7, 8, stride=8), :]
                before = jnp.where(
                    span == 0,
                    pltpu.roll(last, CROSS + 1 - EZN, 1),
                    pltpu.roll(last, 1, 1),
                )
                after = jnp.where(
                    span == EZN - 1,
                    pltpu.roll(first, EZN - 1, 1),
                    pltpu.roll(first, CROSS - 1, 1),
                )
                view[pl.ds(base, 8, stride=8), :] = 0.5 * (first + before)
                view[pl.ds(base + 7, 8, stride=8), :] = 0.5 * (last + after)
            for j in range(8):
                at = pl.ds(base + 8 * j, 8)
                lam[n, at, :] = middle_eigen(*[grad[n, m, at, :] for m in range(9)])
            return carry

        lax.fori_loop(0, 8, plane, 0)

    for n in range(count):
        for o in range(2):

            def along_z(i, carry, n=n, o=o):
                base = i * 64
                points = [lam[n, pl.ds(base + k, 8, stride=8), :] for k in range(8)]
                for w in range(4):
                    total = points[0] * res_z[n][o, w, 0:1, :]
                    for k in range(1, 8):
                        total = total + points[k] * res_z[n][o, w, k : k + 1, :]
                    stage_z[pl.ds(pl.multiple_of(w * 64 + i * 8, 8), 8), :] = total
                return carry

            lax.fori_loop(0, 8, along_z, 0)
            for w in range(4):
                points = [stage_z[pl.ds(w * 64 + j, 8, stride=8), :] for j in range(8)]
                for v in range(4):
                    total = points[0] * res_y[n][o, v, 0:1, :]
                    for j in range(1, 8):
                        total = total + points[j] * res_y[n][o, v, j : j + 1, :]
                    stage_y[32 * v + 8 * w : 32 * v + 8 * w + 8, :] = total
            points = [
                jnp.concatenate(
                    [stage_y[pl.ds(i, 8, stride=8), :], stage_y[pl.ds(64 + i, 8, stride=8), :]], axis=0
                )
                for i in range(8)
            ]
            for u in range(8):
                total = points[0] * res_x[n][o, u, 0:1, :]
                for i in range(1, 8):
                    total = total + points[i] * res_x[n][o, u, i : i + 1, :]
                upper = total.astype(BF)
                lower = (total - upper.astype(F32)).astype(BF)
                at = out_lanes(o, n)
                out_rows[16 * u : 16 * u + 16, at : at + CROSS] = upper
                out_rows[128 + 16 * u : 144 + 16 * u, at : at + CROSS] = lower


def inner_kernel(
    vel1, vel2, opx, opy, opz, inv, x1, x2, y1, y2, z1, z2, prevs, nexts,
    rows, grad, lam, stage_z, stage_y,
):
    slab_layers(
        (1, 2), (vel1, vel2), opx, opy, opz, inv, (x1, x2), (y1, y2), (z1, z2),
        (prevs.at[0], prevs.at[1]), (nexts.at[1], nexts.at[2]),
        rows, lambda o, n: 256 * o + 128 * n, grad, lam, stage_z, stage_y,
    )


def outer_kernel(
    vel0, vel3, opx, opy, opz, inv, x0, x3, y0, y3, z0, z3,
    prev0, prev3, next0, next3, inner_rows, slots, block_rows,
    send, rows, grad, lam, stage_z, stage_y,
):
    slab_layers(
        (0, 3), (vel0, vel3), opx, opy, opz, inv, (x0, x3), (y0, y3), (z0, z3),
        (prev0, prev3.at[0]), (next0.at[0], next3),
        rows, lambda o, n: 512 * o + 384 * n, grad, lam, stage_z, stage_y,
    )
    for o in range(2):
        rows[:, 512 * o + 128 : 512 * o + 384] = inner_rows[:, 256 * o : 256 * o + 256]
    slot_row = jnp.concatenate([slots[0:1, :], slots[1:2, :]], axis=1)

    def pack(g, carry):
        base = pl.multiple_of(g * 16, 16)
        chosen = onehot(iota((256, 1024), 0) + g * 256 == slot_row)
        packed = dot_nt(chosen, rows[...])
        send[pl.ds(base, 16), 0:SLOTS, :] = (packed[:, 0:128] + packed[:, 128:256]).reshape(16, SLOTS, 128)
        send[pl.ds(base, 16), SLOTS, :] = block_rows[pl.ds(base, 16), :]
        return carry

    lax.fori_loop(0, 8, pack, 0)


def exchange_kernel(source, landed, send_sem, recv_sem, own_sem):
    me = lax.axis_index("dom")
    count = lax.axis_size("dom")
    barrier = pltpu.get_barrier_semaphore()

    def greet(step, carry):
        pl.semaphore_signal(
            barrier, inc=1, device_id=(lax.rem(me + step, count),),
            device_id_type=pl.DeviceIdType.MESH,
        )
        return carry

    lax.fori_loop(1, count, greet, 0)
    own = pltpu.make_async_copy(source.at[me], landed.at[me], own_sem)
    own.start()
    pl.semaphore_wait(barrier, count - 1)

    def push(step, carry):
        peer = lax.rem(me + step, count)
        pltpu.make_async_remote_copy(
            src_ref=source.at[peer], dst_ref=landed.at[me], send_sem=send_sem, recv_sem=recv_sem,
            device_id=(peer,), device_id_type=pl.DeviceIdType.MESH,
        ).start()
        return carry

    lax.fori_loop(1, count, push, 0)
    own.wait()
    every = pltpu.make_async_remote_copy(
        src_ref=source.at[pl.ds(0, count - 1)], dst_ref=landed.at[pl.ds(0, count - 1)],
        send_sem=send_sem, recv_sem=recv_sem,
        device_id=(me,), device_id_type=pl.DeviceIdType.MESH,
    )
    every.wait_recv()
    every.wait_send()


def unpack_kernel(landed, bricks, rows, blocks):
    group = pl.program_id(0)

    @pl.when(group == 0)
    def _():
        blocks[...] = jnp.sum(landed[:, SLOTS, :].reshape(16, 8, 128), axis=1).astype(I32)
        for part in range(8):
            values = landed[16 * part : 16 * part + 16, 0:SLOTS, :].reshape(256, 128)
            upper = values.astype(BF)
            rows[256 * part : 256 * part + 256, 0:128] = upper
            rows[256 * part : 256 * part + 256, 128:256] = (values - upper.astype(F32)).astype(BF)

    place = iota((256, 256), 0) + group * 256
    total = None
    for part in range(8):
        named = jnp.concatenate(
            [blocks[2 * part : 2 * part + 1, :], blocks[2 * part + 1 : 2 * part + 2, :]], axis=1
        )
        term = dot(onehot(place == named), rows[256 * part : 256 * part + 256, :])
        total = term if total is None else total + term
    bricks[0] = total[:, 0:128] + total[:, 128:256]


def whole(shape, *indices):
    at = tuple(indices) if indices else (0,) * len(shape)
    return pl.BlockSpec(shape, lambda *_: at)


VLIMIT = pltpu.CompilerParams(vmem_limit_bytes=48 << 20)


def prepare(vel, inv, piece_target, target_brick, target_block, brick_home):
    d = diff_matrix()
    one = np.eye(8)
    opx = np.kron(np.kron(d, one), one)
    opy = np.kron(np.kron(one, d), one)
    opz = np.kron(np.kron(one, one), d)
    opface = np.concatenate([op[rows] for rows in (slice(0, 64), slice(448, 512)) for op in (opx, opy, opz)])
    opface = jnp.asarray(opface, F32).astype(BF)
    face = jax.ShapeDtypeStruct((9, 64, 128), F32)
    faces = jax.ShapeDtypeStruct((3, 9, 64, 128), F32)
    return pl.pallas_call(
        prep_kernel,
        out_shape=(faces, faces, face, face, jax.ShapeDtypeStruct((2, 512), I32),
                   jax.ShapeDtypeStruct((128, 128), F32)),
        compiler_params=VLIMIT,
        name="prep",
    )(vel, opface, inv, piece_target, target_brick.reshape(1, 512), target_block.reshape(1, 512),
      brick_home.reshape(1, 128))


def operators():
    d = diff_matrix()
    one = np.eye(8)
    opx = np.kron(np.kron(d, one), one)
    opy = np.kron(np.kron(np.eye(4), d), one)
    opz = np.kron(np.eye(32), d)
    return [jnp.asarray(op, F32).astype(BF) for op in (opx, opy, opz)]


def layer_specs(layers):
    specs = [whole((3, 512, 128), 0, 0, layer) for layer in layers]
    specs += [whole((512, 512)), whole((256, 256)), whole((256, 256)), whole((3, 512))]
    specs += [whole((2, 8, 8, 128), 0, 0, 0, layer) for layer in layers]
    specs += [whole((2, 4, 8, 128), 0, 0, 0, layer) for _ in range(2) for layer in layers]
    return specs


LAYER_SCRATCH = [
    pltpu.VMEM((2, 9, 512, 128), F32),
    pltpu.VMEM((2, 512, 128), F32),
    pltpu.VMEM((256, 128), F32),
    pltpu.VMEM((128, 128), F32),
]


def layer_args(vel, inv, res_x, res_y, res_z):
    return [vel, vel, *operators(), inv, res_x, res_x, res_y, res_y, res_z, res_z]


def inner(args, high, low):
    return pl.pallas_call(
        inner_kernel,
        grid=(1,),
        in_specs=layer_specs((1, 2)) + [whole((2, 9, 64, 128)), whole((3, 9, 64, 128))],
        out_specs=whole((256, 512)),
        out_shape=jax.ShapeDtypeStruct((256, 512), BF),
        scratch_shapes=LAYER_SCRATCH,
        compiler_params=VLIMIT,
        cost_estimate=pl.CostEstimate(flops=2_000_000_000, bytes_accessed=20_000_000, transcendentals=0),
        name="inner",
    )(*args, high, low)


def outer(args, from_prev, high, low, from_next, inner_rows, slots, block_rows):
    face = whole((9, 64, 128))
    return pl.pallas_call(
        outer_kernel,
        grid=(1,),
        in_specs=layer_specs((0, 3)) + [
            face, whole((1, 9, 64, 128), 2, 0, 0, 0), whole((1, 9, 64, 128)), face,
            whole((256, 512)), whole((2, 512)), whole((128, 128)),
        ],
        out_specs=whole((128, SLOTS + 1, 128)),
        out_shape=jax.ShapeDtypeStruct((128, SLOTS + 1, 128), F32),
        scratch_shapes=[pltpu.VMEM((256, 1024), BF)] + LAYER_SCRATCH,
        compiler_params=VLIMIT,
        cost_estimate=pl.CostEstimate(flops=4_000_000_000, bytes_accessed=20_000_000, transcendentals=0),
        name="outer",
    )(*args, from_prev, high, low, from_next, inner_rows, slots, block_rows)


def exchange(send):
    return pl.pallas_call(
        exchange_kernel,
        out_shape=jax.ShapeDtypeStruct(send.shape, send.dtype),
        in_specs=[pl.BlockSpec(memory_space=pl.ANY)],
        out_specs=pl.BlockSpec(memory_space=pl.ANY),
        scratch_shapes=[pltpu.SemaphoreType.DMA] * 3,
        compiler_params=pltpu.CompilerParams(collective_id=0, has_side_effects=True),
        name="exchange",
    )(send)


def unpack(landed):
    return pl.pallas_call(
        unpack_kernel,
        grid=(8,),
        in_specs=[whole((128, SLOTS + 1, 128))],
        out_specs=pl.BlockSpec((1, 256, 128), lambda g: (0, g, 0)),
        out_shape=jax.ShapeDtypeStruct((1, BLOCKS, 128), F32),
        scratch_shapes=[pltpu.VMEM((2048, 256), BF), pltpu.VMEM((16, 128), I32)],
        compiler_params=VLIMIT,
        name="unpack",
    )(landed)


def shards(
    velocity, inverse_sizes, resample_x, resample_y, resample_z,
    piece_target, target_brick, target_block, brick_home,
):
    count = lax.axis_size("dom")
    low, high, low_rim, high_rim, slots, block_rows = prepare(
        velocity, inverse_sizes, piece_target, target_brick, target_block, brick_home
    )
    from_prev = lax.ppermute(high_rim, "dom", [(i, (i + 1) % count) for i in range(count)])
    from_next = lax.ppermute(low_rim, "dom", [((i + 1) % count, i) for i in range(count)])
    args = layer_args(velocity, inverse_sizes, resample_x, resample_y, resample_z)
    inner_rows = inner(args, high, low)
    send = outer(args, from_prev, high, low, from_next, inner_rows, slots, block_rows)
    return unpack(exchange(send))


def solution(mesh):
    return jax.shard_map(
        shards,
        mesh=mesh,
        in_specs=(
            P(None, None, "dom"),
            P(None, "dom"),
            P(None, None, None, "dom"),
            P(None, None, None, "dom"),
            P(None, None, None, "dom"),
            P(None, "dom"),
            P("dom", None),
            P("dom"),
            P(),
        ),
        out_specs=P("dom", None, None),
        check_vma=False,
    )
```

time: 734 us -> 66.4 us (0.09); the launches traced: 724 us -> 66 us
  matrix products: 394 us -> 0 us
  local copies, waits for them, and re-layouts: 204 us -> 8.4 us
  other arithmetic: 70.8 us -> 0 us
  Pallas kernels: 0 us -> 54.4 us
  waiting for transfers between devices: 28.3 us -> 0.01 us
  starting transfers between devices: 25.3 us -> 3.08 us
    dot_general x4 -> x0, matrix products: 394 us -> none  [the longest x1 273 us: resample(): jnp.einsum('ocke,oabke->oabce', weight_z, along_y, precision=highest)]
    scatter x3 -> x0, local copies, waits for them, and re-layouts: 65.8 us -> none  [the longest x2 61.2 us: stitch_cross(): gradient = gradient.at[:, :, :, 0].set(low_face + from_before).at[:, :, :...]
    pallas_call x0 -> x5, Pallas kernels: none -> 54.4 us  [the longest x1 28.8 us: exchange(): pl.pallas_call(exchange_kernel, out_shape=jax.ShapeDtypeStruct(send.shape...]
    transpose x2 -> x0, local copies, waits for them, and re-layouts: 39.9 us -> none  [the longest x1 33.1 us: resample(): jnp.einsum('oaie,ijke->oajke', weight_x, lambda_two, precision=highest)]
    all_to_all x2 -> x0, waiting for transfers between devices: 28.3 us -> none  [the longest x1 28.3 us: shards(): lax.all_to_all(sendbuf, 'dom', split_axis=0, concat_axis=0, tiled=True)]
    scatter-add x1 -> x0, other arithmetic: 24.7 us -> none  [shards(): brick_image = jnp.zeros((BLOCKS, 128), jnp.float32).at[received_blocks.re...]
    all_to_all x2 -> x0, starting transfers between devices: 22.3 us -> none  [the longest x1 12.1 us: shards(): lax.all_to_all(indices, 'dom', split_axis=0, concat_axis=0, tiled=True)]
    gather x3 -> x0, local copies, waits for them, and re-layouts: 19.9 us -> none  [the longest x2 13 us: shards(): owners = brick_home[target_brick[local_ids, 0]]]
  transfers between devices with their start and end apart: 4 -> 2, of which waited for: 1 -> 0; matrix products, arithmetic and copies ran while one was open for 85% -> 0% of each run, Pallas kernels for 0% -> 12%
where the time goes in v1:
time: 66.4 us; the launch traced here: 66 us
  Pallas kernels  54.4 us (82%)
  local copies, waits for them, and re-layouts  8.4 us (13%)
  starting transfers between devices  3.08 us (5%)
    pallas_call x1, Pallas kernels, exchange(): pl.pallas_call(exchange_kernel, out_shape=jax.ShapeDtypeStruct(send.shape...  28.8 us
    pallas_call x1, Pallas kernels, outer(): pl.pallas_call(outer_kernel, grid=(1,), in_specs=layer_specs((0, 3)) + [f...  11.4 us
    unnamed x32, local copies, waits for them, and re-layouts  8.4 us
    pallas_call x1, Pallas kernels, inner(): pl.pallas_call(inner_kernel, grid=(1,), in_specs=layer_specs((1, 2)) + [w...  7.65 us
    pallas_call x1, Pallas kernels, unpack(): pl.pallas_call(unpack_kernel, grid=(8,), in_specs=[whole((128, SLOTS + 1,...  5.08 us
    ppermute x1, starting transfers between devices, shards(): lax.ppermute(high_rim, 'dom', [(i, (i + 1) % count) for i in range(count)])  3.08 us
    pallas_call x1, Pallas kernels, prepare(): pl.pallas_call(prep_kernel, out_shape=(faces, faces, face, face, jax.Shap...  1.42 us
  transfers between devices with their start and end apart: 2, of which 0 were waited for; matrix products, arithmetic and copies ran while one was open for 0% of the time, Pallas kernels for 12%

profile of v1, /device:TPU:1, one launch (start us, length us, event | category | flops | bytes accessed | tf_op | source)
XLA Modules:
  0.0 66.0 jit_solution(18360044722679461300)
XLA Ops:
  0.0 0.0 copy-start.2
  0.0 1.4 %copy-done.2 = bf16[3,512,512]{2,1,0:T(8,128)(2,1)S(1)} copy-done((bf16[3,512,512]{2,1,0:T(8,128)(2,1)S(1)}, bf16[3,512,512]{2,1,0:T(8,128)(2,1)}, u32[]{:S(2)}) %copy-start.2) | copy-done | bytes 1572888
  1.4 0.0 copy-start.3
  1.4 1.0 %copy-done.3 = bf16[384,512]{1,0:T(8,128)(2,1)S(1)} copy-done((bf16[384,512]{1,0:T(8,128)(2,1)S(1)}, bf16[384,512]{1,0:T(8,128)(2,1)}, u32[]{:S(2)}) %copy-start.3) | copy-done | bytes 393240
  2.4 0.7 %copy-done.4 = f32[3,512]{1,0:T(4,128)S(1)} copy-done((f32[3,512]{1,0:T(4,128)S(1)}, f32[3,512]{1,0:T(4,128)}, u32[]{:S(2)}) %copy-start.4) | copy-done | bytes 6168
  3.1 0.7 %copy-done.6 = s32[2,512]{1,0:T(2,128)S(1)} copy-done((s32[2,512]{1,0:T(2,128)S(1)}, s32[2,512]{1,0:T(2,128)}, u32[]{:S(2)}) %copy-start.6) | copy-done | bytes 4120
  3.8 0.7 %copy-done.7 = s32[512,1]{0,1:T(1,128)S(1)} copy-done((s32[512,1]{0,1:T(1,128)S(1)}, s32[512,1]{0,1:T(1,128)}, u32[]{:S(2)}) %copy-start.7) | copy-done | bytes 2072
  4.5 0.7 %copy-done.8 = s32[512]{0:T(512)S(1)} copy-done((s32[512]{0:T(512)S(1)}, s32[512]{0:T(512)}, u32[]{:S(2)}) %copy-start.8) | copy-done | bytes 2072
  5.2 0.7 copy-done.9
  5.8 0.0 copy-start.13
  5.8 0.0 copy-start.14
  5.8 0.0 copy-start.15
  5.9 1.4 %prep.1 = (f32[3,9,64,128]{3,2,1,0:T(8,128)S(1)}, f32[3,9,64,128]{3,2,1,0:T(8,128)S(1)}, f32[9,64,128]{2,1,0:T(8,128)S(1)}, f32[9,64,128]{2,1,0:T(8,128)S(1)}, s...) custom-call(bf16[3,512,512]{2,1,0:T(8,128)(2,1)S(1)} %copy-done.2, bf16[384,512]{1,0:T(8,128)(2,1)S(1)} %copy-done.3, ...), custom_call_target="tpu_custom_call" | custom-call | tf_op jit(solution)/shard_map/prep/pallas_call | solution.py:372
  7.3 3.1 %collective-permute-start = (f32[9,64,128]{2,1,0:T(8,128)S(1)}, f32[9,64,128]{2,1,0:T(8,128)S(1)}, u32[]{:S(2)}, u32[]{:S(2)}) collective-permute-start(f32[9,64,128]{2,1,0:T(8,128)S(1)} %get-tuple-element.11), channel_id=1, source_target_pairs={{0,1},{1,2},{2,3},{3,4},{4,5},{5,6},{6,7},{7,8},{8,9},{9,10},{10,1... | collective-permute-start | bytes 884744 | tf_op jit(solution)/shard_map/ppermute | solution.py:476
  10.4 0.0 collective-permute-start.1
  10.4 0.0 copy-done.5
  10.4 0.0 copy-done.10
  10.4 0.0 copy-done.11
  10.4 0.0 copy-done.12
  10.4 0.0 copy-done.13
  10.4 0.0 copy-done.14
  10.4 0.0 copy-done.15
  10.4 7.7 %inner.1.inner_rows = bf16[256,512]{1,0:T(8,128)(2,1)S(1)} custom-call(bf16[3,512,512]{2,1,0:T(8,128)(2,1)S(1)} %copy-done.2, bf16[3,512,512]{2,1,0:T(8,128)(2,1)S(1)} %copy-done.2, bf16[512,512]{1,0:T(8,128)(2,1)S(1)} %copy-done.13, bf16[256,256]{1,0:T(8,128)(2,1)S(1)} %copy-done.15, bf16[256,256]{1,0:T(8,128)(2,1)S(1)} %copy-done.14, ...), custom_call_target="tpu_custom_call" | custom-call | flops 2000000000 | bytes 20000000 | tf_op jit(solution)/shard_map/inner/pallas_call | solution.py:412
  18.1 0.0 collective-permute-done.prev0
  18.1 0.0 collective-permute-done.1.next3
  18.1 11.4 %outer.1.source = f32[128,17,128]{2,1,0:T(8,128)S(1)} custom-call(bf16[3,512,512]{2,1,0:T(8,128)(2,1)} %vel3.1, bf16[3,512,512]{2,1,0:T(8,128)(2,1)} %vel3.1, bf16[512,512]{1,0:T(8,128)(2,1)S(1)} %copy-done.13, bf16[256,256]{1,0:T(8,128)(2,1)S(1)} %copy-done.15, bf16[256,256]{1,0:T(8,128)(2,1)S(1)} %copy-done.14, f32[3,512]{1,0:T(4,128)S(1)} %copy-done.5, ...), custom_call_target="tpu_custom_call" | custom-call | flops 4000000000 | bytes 20000000 | tf_op jit(solution)/shard_map/outer/pallas_call | solution.py:427
  29.5 0.0 copy-start.1
  29.6 1.2 %copy-done.1 = f32[128,17,128]{2,1,0:T(8,128)} copy-done((f32[128,17,128]{2,1,0:T(8,128)}, f32[128,17,128]{2,1,0:T(8,128)S(1)}, u32[]{:S(2)}) %copy-start.1) | copy-done | bytes 1114136
  30.7 28.8 %exchange.1.landed = f32[128,17,128]{2,1,0:T(8,128)} custom-call(f32[128,17,128]{2,1,0:T(8,128)} %copy-done.1), custom_call_target="tpu_custom_call" | custom-call | tf_op jit(solution)/shard_map/exchange/pallas_call | solution.py:444
  59.5 0.0 copy-start
  59.5 1.4 %copy-done = f32[128,17,128]{2,1,0:T(8,128)S(1)} copy-done((f32[128,17,128]{2,1,0:T(8,128)S(1)}, f32[128,17,128]{2,1,0:T(8,128)}, u32[]{:S(2)}) %copy-start) | copy-done | bytes 1114136
  60.9 5.1 %unpack.1 = f32[1,2048,128]{2,1,0:T(8,128)} custom-call(f32[128,17,128]{2,1,0:T(8,128)S(1)} %copy-done), custom_call_target="tpu_custom_call" | custom-call | tf_op jit(solution)/shard_map/unpack/pallas_call | solution.py:456
  (9 shorter events, 0.0 us)
Async XLA Ops:
  0.0 1.4 %copy-start.2 = (bf16[3,512,512]{2,1,0:T(8,128)(2,1)S(1)}, bf16[3,512,512]{2,1,0:T(8,128)(2,1)}, u32[]{:S(2)}) copy-start(bf16[3,512,512]{2,1,0:T(8,128)(2,1)} %vel3.1) | copy-start | bytes 4718596
  1.4 1.0 %copy-start.3 = (bf16[384,512]{1,0:T(8,128)(2,1)S(1)}, bf16[384,512]{1,0:T(8,128)(2,1)}, u32[]{:S(2)}) copy-start(bf16[384,512]{1,0:T(8,128)(2,1)} %constant.15.opface) | copy-start | bytes 1179652
  2.4 0.7 %copy-start.4 = (f32[3,512]{1,0:T(4,128)S(1)}, f32[3,512]{1,0:T(4,128)}, u32[]{:S(2)}) copy-start(f32[3,512]{1,0:T(4,128)} %inv.5) | copy-start | bytes 18436
  3.1 0.7 %copy-start.6 = (s32[2,512]{1,0:T(2,128)S(1)}, s32[2,512]{1,0:T(2,128)}, u32[]{:S(2)}) copy-start(s32[2,512]{1,0:T(2,128)} %target_of.1) | copy-start | bytes 12292
  3.8 0.7 %copy-start.7 = (s32[512,1]{0,1:T(1,128)S(1)}, s32[512,1]{0,1:T(1,128)}, u32[]{:S(2)}) copy-start(s32[512,1]{0,1:T(1,128)} %param.19) | copy-start | bytes 6148
  4.5 0.7 %copy-start.8 = (s32[512]{0:T(512)S(1)}, s32[512]{0:T(512)}, u32[]{:S(2)}) copy-start(s32[512]{0:T(512)} %param.20) | copy-start | bytes 6148
  5.2 0.7 copy-start.9
  5.8 4.6 %copy-start.5 = (f32[3,512]{1,0:T(4,128)S(1)}, f32[3,512]{1,0:T(4,128)}, u32[]{:S(2)}) copy-start(f32[3,512]{1,0:T(4,128)} %inv.5) | copy-start | bytes 18436
  5.8 4.6 %copy-start.10 = (f32[2,8,8,512]{3,2,1,0:T(8,128)S(1)}, f32[2,8,8,512]{3,2,1,0:T(8,128)}, u32[]{:S(2)}) copy-start(f32[2,8,8,512]{3,2,1,0:T(8,128)} %x3.1) | copy-start | bytes 786436
  5.8 4.6 %copy-start.11 = (f32[2,4,8,512]{3,2,1,0:T(8,128)S(1)}, f32[2,4,8,512]{3,2,1,0:T(8,128)}, u32[]{:S(2)}) copy-start(f32[2,4,8,512]{3,2,1,0:T(8,128)} %y3.1) | copy-start | bytes 393220
  5.8 4.6 %copy-start.12 = (f32[2,4,8,512]{3,2,1,0:T(8,128)S(1)}, f32[2,4,8,512]{3,2,1,0:T(8,128)}, u32[]{:S(2)}) copy-start(f32[2,4,8,512]{3,2,1,0:T(8,128)} %z3.1) | copy-start | bytes 393220
  5.8 4.6 %copy-start.13 = (bf16[512,512]{1,0:T(8,128)(2,1)S(1)}, bf16[512,512]{1,0:T(8,128)(2,1)}, u32[]{:S(2)}) copy-start(bf16[512,512]{1,0:T(8,128)(2,1)} %constant.12.opx) | copy-start | bytes 1572868
  5.8 4.6 %copy-start.14 = (bf16[256,256]{1,0:T(8,128)(2,1)S(1)}, bf16[256,256]{1,0:T(8,128)(2,1)}, u32[]{:S(2)}) copy-start(bf16[256,256]{1,0:T(8,128)(2,1)} %constant.14.opz) | copy-start | bytes 393220
  5.8 4.6 %copy-start.15 = (bf16[256,256]{1,0:T(8,128)(2,1)S(1)}, bf16[256,256]{1,0:T(8,128)(2,1)}, u32[]{:S(2)}) copy-start(bf16[256,256]{1,0:T(8,128)(2,1)} %constant.13.opy) | copy-start | bytes 393220
  7.3 10.8 %collective-permute-start = (f32[9,64,128]{2,1,0:T(8,128)S(1)}, f32[9,64,128]{2,1,0:T(8,128)S(1)}, u32[]{:S(2)}, u32[]{:S(2)}) collective-permute-start(f32[9,64,128]{2,1,0:T(8,128)S(1)} %get-tuple-element.11), channel_id=1, source_target_pairs={{0,1},{1,2},{2,3},{3,4},{4,5},{5,6},{6,7},{7,8},{8,9},{9,10},{10,1... | collective-permute-start | bytes 884744 | tf_op jit(solution)/shard_map/ppermute | solution.py:476
  10.4 7.7 %collective-permute-start.1 = (f32[9,64,128]{2,1,0:T(8,128)S(1)}, f32[9,64,128]{2,1,0:T(8,128)S(1)}, u32[]{:S(2)}, u32[]{:S(2)}) collective-permute-start(f32[9,64,128]{2,1,0:T(8,128)S(1)} %get-tuple-element.14), channel_id=1, source_target_pairs={{1,0},{2,1},{3,2},{4,3},{5,4},{6,5},{7,6},{8,7},{9,8},{10,9},{11,1... | collective-permute-start | bytes 884744 | tf_op jit(solution)/shard_map/ppermute | solution.py:477
  29.5 1.2 %copy-start.1 = (f32[128,17,128]{2,1,0:T(8,128)}, f32[128,17,128]{2,1,0:T(8,128)S(1)}, u32[]{:S(2)}) copy-start(f32[128,17,128]{2,1,0:T(8,128)S(1)} %outer.1.source) | copy-start | bytes 3342340
  59.5 1.4 %copy-start = (f32[128,17,128]{2,1,0:T(8,128)S(1)}, f32[128,17,128]{2,1,0:T(8,128)}, u32[]{:S(2)}) copy-start(f32[128,17,128]{2,1,0:T(8,128)} %exchange.1.landed) | copy-start | bytes 3342340

commit v2 on v1

v2 whole, which is shorter than its diff:
```python
import jax
import jax.numpy as jnp
import numpy as np
from jax import lax
from jax.experimental import pallas as pl
from jax.experimental.pallas import tpu as pltpu
from jax.sharding import PartitionSpec as P

EYN = 8
EZN = 16
BLOCKS = 2048
CROSS = 128
LAYERS = 4
SLOTS = 16
BF = jnp.bfloat16
F32 = jnp.float32
I32 = jnp.int32

GLL_NODES = [
    -1.0,
    -0.8717401485096066,
    -0.5917001814331423,
    -0.2092992179024789,
    0.2092992179024789,
    0.5917001814331423,
    0.8717401485096066,
    1.0,
]

SINE_POLY = (
    0.6666666865348816,
    -0.2716042101383209,
    0.18378925323486328,
    -0.1428457647562027,
    0.11690858751535416,
    -0.09370578080415726,
    0.06620869785547256,
    -0.03593844175338745,
    0.012577426619827747,
    -0.002056414494290948,
)


def diff_matrix():
    nodes = GLL_NODES
    weights = []
    for first in range(8):
        product_term = 1.0
        for other in range(8):
            if other != first:
                product_term = product_term * (nodes[first] - nodes[other])
        weights.append(1.0 / product_term)
    rows = []
    for first in range(8):
        row = []
        for second in range(8):
            if second == first:
                row.append(0.0)
            else:
                row.append(weights[second] / weights[first] / (nodes[first] - nodes[second]))
        row[first] = -sum(row)
        rows.append(row)
    return np.array(rows)


def iota(shape, dim):
    return lax.broadcasted_iota(I32, shape, dim)


def onehot(mask):
    return jnp.where(mask, 1.0, 0.0).astype(BF)


def dot(a, b):
    return jnp.dot(a, b, preferred_element_type=F32)


def dot_nt(a, b):
    return lax.dot_general(a, b, (((1,), (1,)), ((), ())), preferred_element_type=F32)


def route(target_of, brick_of, block_of, home_of, slots, block_rows):
    me = lax.axis_index("dom")
    same = iota((128, 512), 0) == brick_of[...]
    member = onehot(same)
    earlier = onehot(iota((512, 512), 0) < iota((512, 512), 1))
    ordinal = jnp.sum(jnp.where(same, dot(member, earlier), 0.0), axis=0, keepdims=True)
    homes = jnp.broadcast_to(home_of[...].astype(F32), (8, 128)).astype(BF)
    home = dot(homes, member)[0:1]
    row = iota((8, 512), 0)
    pair = jnp.where(row == 0, home, jnp.where(row == 1, ordinal, 0.0)).astype(BF)
    for o in range(2):
        chosen = onehot(iota((512, 512), 0) == target_of[o : o + 1, :])
        picked = dot(pair, chosen)
        slots[o : o + 1, :] = (picked[0:1] * SLOTS + picked[1:2]).astype(I32)
    to_home = onehot(iota((128, 512), 0) == home.astype(I32))
    lane = ordinal.astype(I32) + SLOTS * lax.rem(me, 8)
    at_lane = iota((128, 512), 0) == lane
    block = block_of[...]
    upper = jnp.where(at_lane, (block // 16).astype(F32), 0.0).astype(BF)
    lower = jnp.where(at_lane, (block % 16).astype(F32), 0.0).astype(BF)
    block_rows[...] = dot_nt(to_home, upper) * 16.0 + dot_nt(to_home, lower)


def middle_eigen(j00, j01, j02, j10, j11, j12, j20, j21, j22):
    p01 = j01 * j10
    p02 = j02 * j20
    p12 = j12 * j21
    m00 = j00 * j00 + p01 + p02
    m11 = j11 * j11 + p01 + p12
    m22 = j22 * j22 + p02 + p12
    m01 = 0.5 * ((j00 + j11) * (j01 + j10) + j02 * j21 + j12 * j20)
    m02 = 0.5 * ((j00 + j22) * (j02 + j20) + j01 * j12 + j21 * j10)
    m12 = 0.5 * ((j11 + j22) * (j12 + j21) + j10 * j02 + j20 * j01)
    q = (m00 + m11 + m22) * (1.0 / 3.0)
    a00 = m00 - q
    a11 = m11 - q
    a22 = m22 - q
    s01 = m01 * m01
    s02 = m02 * m02
    s12 = m12 * m12
    s = (a00 * a00 + a11 * a11 + a22 * a22) * (1.0 / 6.0) + (s01 + s02 + s12) * (1.0 / 3.0)
    det = a00 * (a11 * a22 - s12) - a11 * s02 - a22 * s01 + 2.0 * (m01 * m02 * m12)
    h = 0.5 * det
    root = jnp.sqrt(s)
    disc = jnp.maximum(s * s * s - h * h, 0.0)
    z = h / jnp.maximum(s * root + jnp.sqrt(disc), 1e-37)
    w = z * z
    poly = SINE_POLY[-1]
    for coefficient in SINE_POLY[-2::-1]:
        poly = poly * w + coefficient
    return q - 2.0 * root * (z * poly)


def stitch_plane(grad, layer, base):
    lane = iota((8, CROSS), 1)
    normal = lane // EZN
    span = lane % EZN
    for m in range(9):
        view = grad.at[layer, m]
        first = view[pl.ds(base, 8), :]
        last = view[pl.ds(base + 56, 8), :]
        view[pl.ds(base, 8), :] = jnp.where(
            normal > 0, 0.5 * (first + pltpu.roll(last, EZN, 1)), first
        )
        view[pl.ds(base + 56, 8), :] = jnp.where(
            normal < EYN - 1, 0.5 * (last + pltpu.roll(first, CROSS - EZN, 1)), last
        )
    for m in range(9):
        view = grad.at[layer, m]
        first = view[pl.ds(base, 8, stride=8), :]
        last = view[pl.ds(base + 7, 8, stride=8), :]
        before = jnp.where(
            span == 0, pltpu.roll(last, CROSS + 1 - EZN, 1), pltpu.roll(last, 1, 1)
        )
        after = jnp.where(
            span == EZN - 1, pltpu.roll(first, EZN - 1, 1), pltpu.roll(first, CROSS - 1, 1)
        )
        view[pl.ds(base, 8, stride=8), :] = 0.5 * (first + before)
        view[pl.ds(base + 7, 8, stride=8), :] = 0.5 * (last + after)


def resample(layer, o, lam, res_x, res_y, res_z, rows, stage_z, stage_y):
    lanes = pl.ds(pl.multiple_of(layer * CROSS, CROSS), CROSS)

    def along_z(i, carry):
        base = i * 64
        points = [lam[layer, pl.ds(base + k, 8, stride=8), :] for k in range(8)]
        for w in range(4):
            total = points[0] * res_z[o, w, 0:1, lanes]
            for k in range(1, 8):
                total = total + points[k] * res_z[o, w, k : k + 1, lanes]
            stage_z[pl.ds(pl.multiple_of(w * 64 + i * 8, 8), 8), :] = total
        return carry

    lax.fori_loop(0, 8, along_z, 0)
    for w in range(4):
        points = [stage_z[pl.ds(w * 64 + j, 8, stride=8), :] for j in range(8)]
        for v in range(4):
            total = points[0] * res_y[o, v, 0:1, lanes]
            for j in range(1, 8):
                total = total + points[j] * res_y[o, v, j : j + 1, lanes]
            stage_y[32 * v + 8 * w : 32 * v + 8 * w + 8, :] = total
    points = [
        jnp.concatenate(
            [stage_y[pl.ds(i, 8, stride=8), :], stage_y[pl.ds(64 + i, 8, stride=8), :]], axis=0
        )
        for i in range(8)
    ]
    at = pl.ds(pl.multiple_of(o * 512 + layer * CROSS, CROSS), CROSS)
    for u in range(8):
        total = points[0] * res_x[o, u, 0:1, lanes]
        for i in range(1, 8):
            total = total + points[i] * res_x[o, u, i : i + 1, lanes]
        upper = total.astype(BF)
        rows[16 * u : 16 * u + 16, at] = upper
        rows[128 + 16 * u : 144 + 16 * u, at] = (total - upper.astype(F32)).astype(BF)


def front_kernel(
    vel_h, face_op_h, inv_h, op_x_h, op_yz_h, target_h, brick_h, block_h, home_h, x_h, y_h, z_h,
    rows, slots, block_rows,
    vel, face_op, inv, op_x, op_yz, target_of, brick_of, block_of, home_of, res_x, res_y, res_z,
    rims, halo, grad, lam, stage_z, stage_y, load_sems, send_sems, recv_sems,
):
    me = lax.axis_index("dom")
    count = lax.axis_size("dom")
    after, before = lax.rem(me + 1, count), lax.rem(me + count - 1, count)
    barrier = pltpu.get_barrier_semaphore()
    for peer in (before, after):
        pl.semaphore_signal(barrier, inc=1, device_id=(peer,), device_id_type=pl.DeviceIdType.MESH)
    remote = (vel_h, face_op_h, inv_h, op_x_h, op_yz_h, target_h, brick_h, block_h, home_h, x_h, y_h, z_h)
    local = (vel, face_op, inv, op_x, op_yz, target_of, brick_of, block_of, home_of, res_x, res_y, res_z)
    loads = [pltpu.make_async_copy(r, l, load_sems.at[n]) for n, (r, l) in enumerate(zip(remote, local))]
    for load in loads:
        load.start()

    for load in loads[:3]:
        load.wait()
    for side, layer in ((0, 0), (1, LAYERS - 1)):
        lanes = slice(CROSS * layer, CROSS * layer + CROSS)
        columns = jnp.concatenate([vel[c, :, lanes] for c in range(3)], axis=1)
        faces = dot(face_op[192 * side : 192 * side + 192, :], columns)
        for c in range(3):
            for a in range(3):
                part = faces[64 * a : 64 * a + 64, CROSS * c : CROSS * c + CROSS]
                rims[side, 3 * c + a] = part * inv[a : a + 1, lanes]

    for load in loads[5:9]:
        load.wait()
    route(target_of, brick_of, block_of, home_of, slots, block_rows)

    pl.semaphore_wait(barrier, 2)
    sends = [
        pltpu.make_async_remote_copy(
            src_ref=rims.at[side], dst_ref=halo.at[1 - side],
            send_sem=send_sems.at[side], recv_sem=recv_sems.at[1 - side],
            device_id=(peer,), device_id_type=pl.DeviceIdType.MESH,
        )
        for side, peer in ((0, before), (1, after))
    ]
    for send in sends:
        send.start()

    for load in loads[3:5]:
        load.wait()
    for c in range(3):
        along_x = dot(op_x[...], vel[c])
        for layer in range(LAYERS):
            lanes = slice(CROSS * layer, CROSS * layer + CROSS)
            grad[layer, 3 * c] = along_x[:, lanes] * inv[0:1, lanes]
        for half in range(2):
            both = dot(op_yz[...], vel[c, 256 * half : 256 * half + 256, :])
            for a in (1, 2):
                for layer in range(LAYERS):
                    lanes = slice(CROSS * layer, CROSS * layer + CROSS)
                    grad[layer, 3 * c + a, 256 * half : 256 * half + 256, :] = (
                        both[256 * a - 256 : 256 * a, lanes] * inv[a : a + 1, lanes]
                    )
    for layer in range(LAYERS - 1):
        for m in range(9):
            mean = 0.5 * (grad[layer, m, 448:512, :] + grad[layer + 1, m, 0:64, :])
            grad[layer, m, 448:512, :] = mean
            grad[layer + 1, m, 0:64, :] = mean

    def plane_of(layer_of):
        def plane(t, carry):
            layer = layer_of(t // 8)
            base = pl.multiple_of(lax.rem(t, 8) * 64, 64)
            stitch_plane(grad, layer, base)
            for j in range(8):
                at = pl.ds(base + 8 * j, 8)
                lam[layer, at, :] = middle_eigen(*[grad[layer, m, at, :] for m in range(9)])
            return carry

        return plane

    def resample_of(layer_of):
        def both(n, carry):
            for o in range(2):
                resample(layer_of(n), o, lam, res_x, res_y, res_z, rows, stage_z, stage_y)
            return carry

        return both

    lax.fori_loop(0, 16, plane_of(lambda n: n + 1), 0)
    for load in loads[9:]:
        load.wait()
    lax.fori_loop(0, 2, resample_of(lambda n: n + 1), 0)
    for send in sends:
        send.wait_recv()
    for m in range(9):
        grad[0, m, 0:64, :] = 0.5 * (grad[0, m, 0:64, :] + halo[0, m])
        grad[LAYERS - 1, m, 448:512, :] = 0.5 * (grad[LAYERS - 1, m, 448:512, :] + halo[1, m])
    lax.fori_loop(0, 16, plane_of(lambda n: n * (LAYERS - 1)), 0)
    lax.fori_loop(0, 2, resample_of(lambda n: n * (LAYERS - 1)), 0)
    for send in sends:
        send.wait_send()


def back_kernel(rows, slots, block_rows, bricks, source, landed, send_sem, recv_sems, own_sem):
    me = lax.axis_index("dom")
    count = lax.axis_size("dom")
    mine = me // 16
    barrier = pltpu.get_barrier_semaphore()

    def greet(step, carry):
        pl.semaphore_signal(
            barrier, inc=1, device_id=(lax.rem(me + step, count),),
            device_id_type=pl.DeviceIdType.MESH,
        )
        return carry

    lax.fori_loop(1, count, greet, 0)
    slot_row = jnp.concatenate([slots[0:1, :], slots[1:2, :]], axis=1)

    def pack(g, carry):
        base = pl.multiple_of(g * 16, 16)
        chosen = onehot(iota((256, 1024), 0) + g * 256 == slot_row)
        packed = dot_nt(chosen, rows[...])
        source[pl.ds(base, 16), 0:SLOTS, :] = (packed[:, 0:128] + packed[:, 128:256]).reshape(16, SLOTS, 128)
        source[pl.ds(base, 16), SLOTS, :] = block_rows[pl.ds(base, 16), :]
        return carry

    lax.fori_loop(0, 8, pack, 0)
    pl.semaphore_wait(barrier, count - 1)

    def push(step, carry):
        peer = lax.rem(me + step, count)
        pltpu.make_async_remote_copy(
            src_ref=source.at[peer], dst_ref=landed.at[me], send_sem=send_sem, recv_sem=recv_sems.at[mine],
            device_id=(peer,), device_id_type=pl.DeviceIdType.MESH,
        ).start()
        return carry

    lax.fori_loop(1, count, push, 0)
    own = pltpu.make_async_copy(source.at[me], landed.at[me], own_sem)
    own.start()
    own.wait()

    def arrived(chunk, number):
        part = landed.at[pl.ds(0, number)]
        pltpu.make_async_remote_copy(
            src_ref=part, dst_ref=part, send_sem=send_sem, recv_sem=recv_sems.at[chunk],
            device_id=(me,), device_id_type=pl.DeviceIdType.MESH,
        ).wait_recv()

    def unpack(chunk, first):
        base = pl.multiple_of(chunk * 16, 16)
        block = jnp.sum(landed[pl.ds(base, 16), SLOTS, :].reshape(2, 8, 128), axis=1).astype(I32)
        named = jnp.concatenate([block[0:1], block[1:2]], axis=1)
        values = landed[pl.ds(base, 16), 0:SLOTS, :].reshape(256, 128)
        upper = values.astype(BF)
        lower = (values - upper.astype(F32)).astype(BF)
        both = jnp.concatenate([upper, lower], axis=1)
        for part in range(8):
            term = dot(onehot(iota((256, 256), 0) + 256 * part == named), both)
            term = term[:, 0:128] + term[:, 128:256]
            at = slice(256 * part, 256 * part + 256)
            bricks[0, at, :] = term if first else bricks[0, at, :] + term

    arrived(mine, 15)
    unpack(mine, True)

    def receive(step, carry):
        chunk = lax.rem(mine + 8 - step, 8)
        arrived(chunk, 16)
        unpack(chunk, False)
        return carry

    lax.fori_loop(1, 8, receive, 0)
    everything = source.at[pl.ds(0, count - 1)]
    pltpu.make_async_remote_copy(
        src_ref=everything, dst_ref=everything, send_sem=send_sem, recv_sem=recv_sems.at[0],
        device_id=(me,), device_id_type=pl.DeviceIdType.MESH,
    ).wait_send()


ANYWHERE = pl.BlockSpec(memory_space=pl.ANY)
IN_VMEM = pl.BlockSpec(memory_space=pltpu.VMEM)


def operators():
    d = diff_matrix()
    one = np.eye(8)
    op_x = np.kron(np.kron(d, one), one)
    op_y = np.kron(np.kron(one, d), one)
    op_z = np.kron(np.kron(one, one), d)
    face = np.concatenate([op[rows] for rows in (slice(0, 64), slice(448, 512)) for op in (op_x, op_y, op_z)])
    op_yz = np.concatenate([op_y[:256, :256], op_z[:256, :256]])
    return [jnp.asarray(op, F32).astype(BF) for op in (face, op_x, op_yz)]


def front(velocity, inverse_sizes, resample_x, resample_y, resample_z, piece_target, target_brick, target_block, brick_home):
    face_op, op_x, op_yz = operators()
    operands = (
        velocity, face_op, inverse_sizes, op_x, op_yz,
        piece_target, target_brick.reshape(1, 512), target_block.reshape(1, 512), brick_home.reshape(1, 128),
        resample_x, resample_y, resample_z,
    )
    scratch = [pltpu.VMEM(array.shape, array.dtype) for array in operands]
    scratch += [
        pltpu.VMEM((2, 9, 64, 128), F32),
        pltpu.VMEM((2, 9, 64, 128), F32),
        pltpu.VMEM((LAYERS, 9, 512, 128), F32),
        pltpu.VMEM((LAYERS, 512, 128), F32),
        pltpu.VMEM((256, 128), F32),
        pltpu.VMEM((128, 128), F32),
        pltpu.SemaphoreType.DMA((len(operands),)),
        pltpu.SemaphoreType.DMA((2,)),
        pltpu.SemaphoreType.DMA((2,)),
    ]
    return pl.pallas_call(
        front_kernel,
        in_specs=[ANYWHERE] * len(operands),
        out_specs=(IN_VMEM,) * 3,
        out_shape=(
            jax.ShapeDtypeStruct((256, 1024), BF),
            jax.ShapeDtypeStruct((2, 512), I32),
            jax.ShapeDtypeStruct((128, 128), F32),
        ),
        scratch_shapes=scratch,
        compiler_params=pltpu.CompilerParams(collective_id=0, has_side_effects=True),
        name="front",
    )(*operands)


def back(rows, slots, block_rows):
    buffer = pltpu.VMEM((128, SLOTS + 1, 128), F32)
    return pl.pallas_call(
        back_kernel,
        in_specs=[IN_VMEM] * 3,
        out_specs=IN_VMEM,
        out_shape=jax.ShapeDtypeStruct((1, BLOCKS, 128), F32),
        scratch_shapes=[
            buffer, buffer, pltpu.SemaphoreType.DMA, pltpu.SemaphoreType.DMA((8,)), pltpu.SemaphoreType.DMA,
        ],
        compiler_params=pltpu.CompilerParams(collective_id=1, has_side_effects=True),
        name="back",
    )(rows, slots, block_rows)


def shards(*operands):
    return back(*front(*operands))


def solution(mesh):
    return jax.shard_map(
        shards,
        mesh=mesh,
        in_specs=(
            P(None, None, "dom"),
            P(None, "dom"),
            P(None, None, None, "dom"),
            P(None, None, None, "dom"),
            P(None, None, None, "dom"),
            P(None, "dom"),
            P("dom", None),
            P("dom"),
            P(),
        ),
        out_specs=P("dom", None, None),
        check_vma=False,
    )
```

time: 66.4 us -> 53 us (0.80)
  local copies, waits for them, and re-layouts: 8.4 us -> 2.26 us
  Pallas kernels: 54.4 us -> 50.6 us
  starting transfers between devices: 3.08 us -> 0 us
    unnamed x32 -> x1, local copies, waits for them, and re-layouts: 8.4 us -> 2.26 us
    pallas_call x5 -> x2, Pallas kernels: 54.4 us -> 50.6 us  [the longest x1 31.5 us: back(): pl.pallas_call(back_kernel, in_specs=[IN_VMEM] * 3, out_specs=IN_VMEM, ou...]
    ppermute x2 -> x0, starting transfers between devices: 3.08 us -> none  [the longest x1 3.08 us: shards(): lax.ppermute(high_rim, 'dom', [(i, (i + 1) % count) for i in range(count)])]
  transfers between devices with their start and end apart: 2 -> 0, of which waited for: 0 -> 0; matrix products, arithmetic and copies ran while one was open for 0% -> 0% of each run, Pallas kernels for 12% -> 0%
where the time goes in v2:
time: 53 us; the launch traced here: 52.9 us
  Pallas kernels  50.6 us (95%)
  local copies, waits for them, and re-layouts  2.26 us (4%)
    pallas_call x1, Pallas kernels, back(): pl.pallas_call(back_kernel, in_specs=[IN_VMEM] * 3, out_specs=IN_VMEM, ou...  31.5 us
    pallas_call x1, Pallas kernels, front(): pl.pallas_call(front_kernel, in_specs=[ANYWHERE] * len(operands), out_spe...  19.1 us
    unnamed x1, local copies, waits for them, and re-layouts  2.26 us

profile of v2, /device:TPU:1, one launch (start us, length us, event | category | flops | bytes accessed | tf_op | source)
XLA Modules:
  0.0 52.9 jit_solution(12919242122123080162)
XLA Ops:
  0.0 19.1 %front.1 = (bf16[256,1024]{1,0:T(8,128)(2,1)}, s32[2,512]{1,0:T(2,128)}, f32[128,128]{1,0:T(8,128)}) custom-call(bf16[3,512,512]{2,1,0:T(8,128)(2,1)} %vel_h.1, bf16[384,512]{1,0:T(8,128)(2,1)} %constant.9.face_op_h, f32[3,512]{1,0:T(4,128)} %inv_h.1, bf16[512,512]{1,0:T(8,128)(2,1)} %constant.10.op_x_h, bf16[512,256]{1,0:T(8,128)(2,1)} %constant.11.op_yz_h, ...), custom_call_target="tpu_custom_call" | custom-call | tf_op jit(solution)/shard_map/front/pallas_call | solution.py:413
  19.1 31.5 %back.1 = f32[1,2048,128]{2,1,0:T(8,128)} custom-call(bf16[256,1024]{1,0:T(8,128)(2,1)} %get-tuple-element.8.rows, s32[2,512]{1,0:T(2,128)} %get-tuple-element.9.slots, f32[128,128]{1,0:T(8,128)} %get-tuple-element.10.block_rows), custom_call_target="tpu_custom_call" | custom-call | tf_op jit(solution)/shard_map/back/pallas_call | solution.py:430
  50.6 2.3 %copy.14 = f32[1,2048,128]{2,1,0:T(8,128)} copy(f32[1,2048,128]{2,1,0:T(8,128)} %back.1) | data formatting | bytes 2097152

commit v3 on v2

v3 whole, which is shorter than its diff:
```python
import math

import jax
import jax.numpy as jnp
import numpy as np
from jax import lax
from jax.experimental import pallas as pl
from jax.experimental.pallas import tpu as pltpu
from jax.sharding import PartitionSpec as P

EYN = 8
EZN = 16
BLOCKS = 2048
CROSS = 128
LAYERS = 4
SLOTS = 16
BF = jnp.bfloat16
F32 = jnp.float32
I32 = jnp.int32
VMEM_LIMIT = 60 * 1024 * 1024

GLL_NODES = [
    -1.0,
    -0.8717401485096066,
    -0.5917001814331423,
    -0.2092992179024789,
    0.2092992179024789,
    0.5917001814331423,
    0.8717401485096066,
    1.0,
]

THIRD_POLY = (
    0.28867512941360474,
    -0.16666603088378906,
    0.12827838957309723,
    -0.10773465782403946,
    0.09301131963729858,
    -0.0773678869009018,
    0.0560062974691391,
    -0.03085879236459732,
    0.010898211039602757,
    -0.0017919066594913602,
)


def diff_matrix():
    nodes = GLL_NODES
    weights = []
    for first in range(8):
        product_term = 1.0
        for other in range(8):
            if other != first:
                product_term = product_term * (nodes[first] - nodes[other])
        weights.append(1.0 / product_term)
    rows = []
    for first in range(8):
        row = []
        for second in range(8):
            if second == first:
                row.append(0.0)
            else:
                row.append(weights[second] / weights[first] / (nodes[first] - nodes[second]))
        row[first] = -sum(row)
        rows.append(row)
    return np.array(rows)


def iota(shape, dim):
    return lax.broadcasted_iota(I32, shape, dim)


def onehot(mask):
    return jnp.where(mask, 1.0, 0.0).astype(BF)


def dot(a, b):
    return jnp.dot(a, b, preferred_element_type=F32)


def dot_nt(a, b):
    return lax.dot_general(a, b, (((1,), (1,)), ((), ())), preferred_element_type=F32)


def route(target_of, brick_of, block_of, home_of, slots, block_rows):
    me = lax.axis_index("dom")
    same = iota((128, 512), 0) == brick_of[...]
    member = onehot(same)
    earlier = onehot(iota((512, 512), 0) < iota((512, 512), 1))
    ordinal = jnp.sum(jnp.where(same, dot(member, earlier), 0.0), axis=0, keepdims=True)
    homes = jnp.broadcast_to(home_of[...].astype(F32), (8, 128)).astype(BF)
    home = dot(homes, member)[0:1]
    row = iota((8, 512), 0)
    pair = jnp.where(row == 0, home, jnp.where(row == 1, ordinal, 0.0)).astype(BF)
    for o in range(2):
        chosen = onehot(iota((512, 512), 0) == target_of[o : o + 1, :])
        picked = dot(pair, chosen)
        slots[o : o + 1, :] = (picked[0:1] * SLOTS + picked[1:2]).astype(I32)
    to_home = onehot(iota((128, 512), 0) == home.astype(I32))
    lane = ordinal.astype(I32) + SLOTS * lax.rem(me, 8)
    at_lane = iota((128, 512), 0) == lane
    block = block_of[...]
    upper = jnp.where(at_lane, (block // 16).astype(F32), 0.0).astype(BF)
    lower = jnp.where(at_lane, (block % 16).astype(F32), 0.0).astype(BF)
    block_rows[...] = dot_nt(to_home, upper) * 16.0 + dot_nt(to_home, lower)


def middle_eigen(j00, j01, j02, j10, j11, j12, j20, j21, j22):
    p01 = j01 * j10
    p02 = j02 * j20
    p12 = j12 * j21
    m00 = j00 * j00 + (p01 + p02)
    m11 = j11 * j11 + (p01 + p12)
    m22 = j22 * j22 + (p02 + p12)
    n01 = (j00 + j11) * (j01 + j10) + (j02 * j21 + j12 * j20)
    n02 = (j00 + j22) * (j02 + j20) + (j01 * j12 + j21 * j10)
    n12 = (j11 + j22) * (j12 + j21) + (j10 * j02 + j20 * j01)
    q = (m00 + m11 + m22) * (1.0 / 3.0)
    a00 = m00 - q
    a11 = m11 - q
    a22 = m22 - q
    s01 = n01 * n01
    s02 = n02 * n02
    s12 = n12 * n12
    a00x2 = a00 + a00
    minor = 4.0 * a11 * a22
    s_12 = (a00x2 * a00x2 - minor) + (s01 + s02 + s12)
    det_4 = a00 * (minor - s12) - (a11 * s02 + a22 * s01) + n01 * n02 * n12
    s_12 = jnp.maximum(s_12, 1e-24)
    inverse = lax.rsqrt(s_12)
    ratio = (det_4 * (3.0 * math.sqrt(3.0))) * (inverse * inverse * inverse)
    rest = jnp.maximum(1.0 - ratio * ratio, 1e-30)
    cosine = rest * lax.rsqrt(rest)
    poly = THIRD_POLY[-1]
    for coefficient in THIRD_POLY[-2::-1]:
        poly = poly * cosine + coefficient
    return q - (s_12 * inverse) * (ratio * poly)


def stitch_y(first, last):
    normal = iota((8, CROSS), 1) // EZN
    return (
        jnp.where(normal > 0, 0.5 * (first + pltpu.roll(last, EZN, 1)), first),
        jnp.where(normal < EYN - 1, 0.5 * (last + pltpu.roll(first, CROSS - EZN, 1)), last),
    )


def stitch_z(first, last):
    span = iota((8, CROSS), 1) % EZN
    before = jnp.where(span == 0, pltpu.roll(last, CROSS + 1 - EZN, 1), pltpu.roll(last, 1, 1))
    after = jnp.where(
        span == EZN - 1, pltpu.roll(first, EZN - 1, 1), pltpu.roll(first, CROSS - 1, 1)
    )
    return 0.5 * (first + before), 0.5 * (last + after)


def stitch_plane(grad, layer, firsts, lasts, stitch):
    pairs = [(grad[layer, m, firsts, :], grad[layer, m, lasts, :]) for m in range(9)]
    pairs = [stitch(first, last) for first, last in pairs]
    for m in range(9):
        grad[layer, m, firsts, :] = pairs[m][0]
        grad[layer, m, lasts, :] = pairs[m][1]


def stitch_plane_z(grad, layer, base):
    stitch_plane(grad, layer, pl.ds(base, 8, stride=8), pl.ds(base + 7, 8, stride=8), stitch_z)


def eigen_plane(grad, lam, layer, base):
    for j in range(8):
        at = pl.ds(base + 8 * j, 8)
        lam[layer, at, :] = middle_eigen(*[grad[layer, m, at, :] for m in range(9)])


def resample(layer, o, lam, res_x, res_y, res_z, rows, stage_z, stage_y):
    lanes = pl.ds(pl.multiple_of(layer * CROSS, CROSS), CROSS)

    def along_z(i, carry):
        base = i * 64
        points = [lam[layer, pl.ds(base + k, 8, stride=8), :] for k in range(8)]
        for w in range(4):
            total = points[0] * res_z[o, w, 0:1, lanes]
            for k in range(1, 8):
                total = total + points[k] * res_z[o, w, k : k + 1, lanes]
            stage_z[pl.ds(pl.multiple_of(w * 64 + i * 8, 8), 8), :] = total
        return carry

    lax.fori_loop(0, 8, along_z, 0)
    for w in range(4):
        points = [stage_z[pl.ds(w * 64 + j, 8, stride=8), :] for j in range(8)]
        for v in range(4):
            total = points[0] * res_y[o, v, 0:1, lanes]
            for j in range(1, 8):
                total = total + points[j] * res_y[o, v, j : j + 1, lanes]
            stage_y[32 * v + 8 * w : 32 * v + 8 * w + 8, :] = total
    points = [
        jnp.concatenate(
            [stage_y[pl.ds(i, 8, stride=8), :], stage_y[pl.ds(64 + i, 8, stride=8), :]], axis=0
        )
        for i in range(8)
    ]
    at = pl.ds(pl.multiple_of(o * 512 + layer * CROSS, CROSS), CROSS)
    for u in range(8):
        total = points[0] * res_x[o, u, 0:1, lanes]
        for i in range(1, 8):
            total = total + points[i] * res_x[o, u, i : i + 1, lanes]
        upper = total.astype(BF)
        rows[16 * u : 16 * u + 16, at] = upper
        rows[128 + 16 * u : 144 + 16 * u, at] = (total - upper.astype(F32)).astype(BF)


def differentiate(vel, op_x, op_yz, inv, grad, rims):
    for c in range(3):
        along_x = dot(op_x[...], vel[c])
        halves = [dot(op_yz[...], vel[c, 256 * half : 256 * half + 256, :]) for half in range(2)]
        for a in range(3):
            m = 3 * c + a

            def block(i, layer, a=a):
                lanes = slice(CROSS * layer, CROSS * layer + CROSS)
                if a == 0:
                    rows = along_x[64 * i : 64 * i + 64, lanes]
                else:
                    at = 256 * (a - 1) + 64 * (i % 4)
                    rows = halves[i // 4][at : at + 64, lanes]
                return rows * inv[a : a + 1, lanes]

            rims[0, m] = block(0, 0)
            rims[1, m] = block(7, LAYERS - 1)
            for layer in range(LAYERS):
                for i in range(1, 8):
                    if i == 7 and layer == LAYERS - 1:
                        continue
                    values = block(i, layer)
                    if i == 7:
                        values = 0.5 * (values + block(0, layer + 1))
                    first, last = stitch_y(values[0:8], values[56:64])
                    places = [(layer, 64 * i)] + ([(layer + 1, 0)] if i == 7 else [])
                    for place, base in places:
                        grad[place, m, base : base + 8, :] = first
                        grad[place, m, base + 8 : base + 56, :] = values[8:56]
                        grad[place, m, base + 56 : base + 64, :] = last


def kernel(
    vel_h, inv_h, op_x_h, op_yz_h, target_h, brick_h, block_h, home_h, x_h, y_h, z_h,
    bricks,
    vel, inv, op_x, op_yz, target_of, brick_of, block_of, home_of, res_x, res_y, res_z,
    rims, halo, grad, lam, stage_z, stage_y, rows, slots, block_rows, source, landed,
    load_sems, halo_send, halo_recv, send_sem, recv_sems, own_sem,
):
    me = lax.axis_index("dom")
    count = lax.axis_size("dom")
    mine = me // 16
    mesh_id = pl.DeviceIdType.MESH

    far = (vel_h, inv_h, op_x_h, op_yz_h, target_h, brick_h, block_h, home_h, x_h, y_h, z_h)
    near = (vel, inv, op_x, op_yz, target_of, brick_of, block_of, home_of, res_x, res_y, res_z)
    loads = [pltpu.make_async_copy(f, n, load_sems.at[k]) for k, (f, n) in enumerate(zip(far, near))]
    for load in loads:
        load.start()
    barrier = pltpu.get_barrier_semaphore()

    def greet(step, carry):
        pl.semaphore_signal(
            barrier, inc=1, device_id=(lax.rem(me + step, count),), device_id_type=mesh_id
        )
        return carry

    lax.fori_loop(1, count, greet, 0)
    for load in loads[:4]:
        load.wait()
    differentiate(vel, op_x, op_yz, inv, grad, rims)

    def plane_z(t, carry):
        stitch_plane_z(grad, t // 8, pl.multiple_of(lax.rem(t, 8) * 64, 64))
        return carry

    def plane_eigen(t, carry):
        eigen_plane(grad, lam, t // 8, pl.multiple_of(lax.rem(t, 8) * 64, 64))
        return carry

    lax.fori_loop(1, 31, plane_z, 0)
    for load in loads[4:8]:
        load.wait()
    route(target_of, brick_of, block_of, home_of, slots, block_rows)

    pl.semaphore_wait(barrier, count - 1)
    sends = [
        pltpu.make_async_remote_copy(
            src_ref=rims.at[side], dst_ref=halo.at[1 - side],
            send_sem=halo_send.at[side], recv_sem=halo_recv.at[1 - side],
            device_id=(lax.rem(me + step, count),), device_id_type=mesh_id,
        )
        for side, step in ((0, count - 1), (1, 1))
    ]
    for send in sends:
        send.start()

    lax.fori_loop(1, 31, plane_eigen, 0)
    for load in loads[8:]:
        load.wait()

    def resample_of(layer_of):
        def both(n, carry):
            for o in range(2):
                resample(layer_of(n), o, lam, res_x, res_y, res_z, rows, stage_z, stage_y)
            return carry

        return both

    lax.fori_loop(0, 2, resample_of(lambda n: n + 1), 0)
    for send in sends:
        send.wait_recv()
    for side, layer, base in ((0, 0, 0), (1, LAYERS - 1, 448)):
        for m in range(9):
            grad[layer, m, base : base + 64, :] = 0.5 * (rims[side, m] + halo[side, m])
        stitch_plane(grad, layer, slice(base, base + 8), slice(base + 56, base + 64), stitch_y)
    for layer, base in ((0, 0), (LAYERS - 1, 448)):
        stitch_plane_z(grad, layer, base)
    for layer, base in ((0, 0), (LAYERS - 1, 448)):
        eigen_plane(grad, lam, layer, base)
    lax.fori_loop(0, 2, resample_of(lambda n: n * (LAYERS - 1)), 0)

    slot_row = jnp.concatenate([slots[0:1, :], slots[1:2, :]], axis=1)

    def push(chunk, first):
        def one(step, carry):
            peer = chunk * 16 + lax.rem(me + step, 16)
            pltpu.make_async_remote_copy(
                src_ref=source.at[peer], dst_ref=landed.at[me],
                send_sem=send_sem, recv_sem=recv_sems.at[mine],
                device_id=(peer,), device_id_type=mesh_id,
            ).start()
            return carry

        lax.fori_loop(first, 16, one, 0)

    def pack(g, carry):
        chunk = lax.rem(mine + 1 + g, 8)
        base = pl.multiple_of(chunk * 16, 16)
        chosen = onehot(iota((256, 1024), 0) + chunk * 256 == slot_row)
        packed = dot_nt(chosen, rows[...])
        source[pl.ds(base, 16), 0:SLOTS, :] = (packed[:, 0:128] + packed[:, 128:256]).reshape(16, SLOTS, 128)
        source[pl.ds(base, 16), SLOTS, :] = block_rows[pl.ds(base, 16), :]

        @pl.when(g > 0)
        def _():
            push(lax.rem(mine + g, 8), 0)

        return carry

    lax.fori_loop(0, 8, pack, 0)
    for send in sends:
        send.wait_send()
    push(mine, 1)
    own = pltpu.make_async_copy(source.at[me], landed.at[me], own_sem)
    own.start()
    own.wait()

    def arrived(chunk, number):
        part = landed.at[pl.ds(0, number)]
        pltpu.make_async_remote_copy(
            src_ref=part, dst_ref=part, send_sem=send_sem, recv_sem=recv_sems.at[chunk],
            device_id=(me,), device_id_type=mesh_id,
        ).wait_recv()

    def unpack(chunk):
        base = pl.multiple_of(chunk * 16, 16)
        block = jnp.sum(landed[pl.ds(base, 16), SLOTS, :].reshape(2, 8, 128), axis=1).astype(I32)
        named = jnp.concatenate([block[0:1], block[1:2]], axis=1)
        values = landed[pl.ds(base, 16), 0:SLOTS, :].reshape(256, 128)
        upper = values.astype(BF)
        lower = (values - upper.astype(F32)).astype(BF)
        both = jnp.concatenate([upper, lower], axis=1)
        for part in range(8):
            term = dot(onehot(iota((256, 256), 0) + 256 * part == named), both)
            at = slice(256 * part, 256 * part + 256)
            bricks[0, at, :] += term[:, 0:128] + term[:, 128:256]

    bricks[...] = jnp.zeros_like(bricks)

    def receive(g, carry):
        chunk = lax.rem(mine + 7 - g, 8)
        arrived(chunk, 16)
        unpack(chunk)
        return carry

    lax.fori_loop(0, 7, receive, 0)
    arrived(mine, 15)
    unpack(mine)
    everything = source.at[pl.ds(0, count - 1)]
    pltpu.make_async_remote_copy(
        src_ref=everything, dst_ref=everything, send_sem=send_sem, recv_sem=recv_sems.at[0],
        device_id=(me,), device_id_type=mesh_id,
    ).wait_send()


def operators():
    d = diff_matrix()
    one = np.eye(8)
    op_x = np.kron(np.kron(d, one), one)
    op_y = np.kron(np.kron(np.eye(4), d), one)
    op_z = np.kron(np.eye(32), d)
    return [jnp.asarray(op, F32).astype(BF) for op in (op_x, np.concatenate([op_y, op_z]))]


def shards(velocity, inverse_sizes, resample_x, resample_y, resample_z, piece_target, target_brick, target_block, brick_home):
    op_x, op_yz = operators()
    operands = (
        velocity, inverse_sizes, op_x, op_yz,
        piece_target, target_brick.reshape(1, 512), target_block.reshape(1, 512), brick_home.reshape(1, 128),
        resample_x, resample_y, resample_z,
    )
    scratch = [pltpu.VMEM(array.shape, array.dtype) for array in operands]
    scratch += [
        pltpu.VMEM((2, 9, 64, 128), F32),
        pltpu.VMEM((2, 9, 64, 128), F32),
        pltpu.VMEM((LAYERS, 9, 512, 128), F32),
        pltpu.VMEM((LAYERS, 512, 128), F32),
        pltpu.VMEM((256, 128), F32),
        pltpu.VMEM((128, 128), F32),
        pltpu.VMEM((256, 1024), BF),
        pltpu.VMEM((2, 512), I32),
        pltpu.VMEM((128, 128), F32),
        pltpu.VMEM((128, SLOTS + 1, 128), F32),
        pltpu.VMEM((128, SLOTS + 1, 128), F32),
        pltpu.SemaphoreType.DMA((len(operands),)),
        pltpu.SemaphoreType.DMA((2,)),
        pltpu.SemaphoreType.DMA((2,)),
        pltpu.SemaphoreType.DMA,
        pltpu.SemaphoreType.DMA((8,)),
        pltpu.SemaphoreType.DMA,
    ]
    return pl.pallas_call(
        kernel,
        in_specs=[pl.BlockSpec(memory_space=pltpu.HBM)] * len(operands),
        out_specs=pl.BlockSpec(memory_space=pltpu.VMEM),
        out_shape=jax.ShapeDtypeStruct((1, BLOCKS, 128), F32),
        scratch_shapes=scratch,
        compiler_params=pltpu.CompilerParams(
            collective_id=0, has_side_effects=True, vmem_limit_bytes=VMEM_LIMIT
        ),
        name="step",
    )(*operands)


def solution(mesh):
    return jax.shard_map(
        shards,
        mesh=mesh,
        in_specs=(
            P(None, None, "dom"),
            P(None, "dom"),
            P(None, None, None, "dom"),
            P(None, None, None, "dom"),
            P(None, None, None, "dom"),
            P(None, "dom"),
            P("dom", None),
            P("dom"),
            P(),
        ),
        out_specs=P("dom", None, None),
        check_vma=False,
    )
```

time: 53 us -> 43.2 us (0.82)
  Pallas kernels: 50.6 us -> 40.8 us
    pallas_call x2 -> x1, Pallas kernels: 50.6 us -> 40.8 us  [shards(): pl.pallas_call(kernel, in_specs=[pl.BlockSpec(memory_space=pltpu.HBM)] *...]
where the time goes in v3:
time: 43.2 us; the launch traced here: 43.1 us
  Pallas kernels  40.8 us (94%)
  local copies, waits for them, and re-layouts  2.26 us (5%)
    pallas_call x1, Pallas kernels, shards(): pl.pallas_call(kernel, in_specs=[pl.BlockSpec(memory_space=pltpu.HBM)] *...  40.8 us
    unnamed x1, local copies, waits for them, and re-layouts  2.26 us

profile of v3, /device:TPU:1, one launch (start us, length us, event | category | flops | bytes accessed | tf_op | source)
XLA Modules:
  0.0 43.1 jit_solution(8042816881786827394)
XLA Ops:
  0.0 40.8 %step.1 = f32[1,2048,128]{2,1,0:T(8,128)} custom-call(bf16[3,512,512]{2,1,0:T(8,128)(2,1)} %vel_h.1, f32[3,512]{1,0:T(4,128)} %inv_h.1, bf16[512,512]{1,0:T(8,128)(2,1)} %constant.6.op_x_h, bf16[512,256]{1,0:T(8,128)(2,1)} %constant.7.op_yz_h, s32[2,512]{1,0:T(2,128)} %target_h.1, s32[1,512]{1,0:T(1,128)} %bitcast.3, s32[1,512]{1,0:T(1,128)} %bitcast.4, ...), custom_call_target="tpu_custom_call" | custom-call | tf_op jit(solution)/shard_map/step/pallas_call | solution.py:435
  40.8 2.3 %copy.13 = f32[1,2048,128]{2,1,0:T(8,128)} copy(f32[1,2048,128]{2,1,0:T(8,128)} %step.1) | data formatting | bytes 2097152

commit v4 on v3

--- a/solution.py
+++ b/solution.py
@@ -17,7 +17,7 @@
 BF = jnp.bfloat16
 F32 = jnp.float32
 I32 = jnp.int32
-VMEM_LIMIT = 60 * 1024 * 1024
+VMEM_LIMIT = 40 << 20
 
 GLL_NODES = [
     -1.0,
@@ -42,6 +42,18 @@
     0.010898211039602757,
     -0.0017919066594913602,
 )
+
+
+def far_first():
+    hops = (0, 1, 2, 1)
+    offsets = [np.unravel_index(n, (4, 4, 4, 2)) for n in np.random.RandomState(1).permutation(128)]
+    offsets.sort(key=lambda at: (any(at) == 0, -hops[at[0]] - hops[at[1]] - hops[at[2]]))
+    return [tuple(int(part) for part in at) for at in offsets]
+
+
+OFFSETS = far_first()
+PACKS = ((0, 2), (2, 2), (4, 2), (6, 2))
+GROUPS = ((0, 2), (2, 2), (4, 2), (6, 2))
 
 
 def diff_matrix():
@@ -82,27 +94,34 @@
     return lax.dot_general(a, b, (((1,), (1,)), ((), ())), preferred_element_type=F32)
 
 
-def route(target_of, brick_of, block_of, home_of, slots, block_rows):
-    me = lax.axis_index("dom")
+def torus(index):
+    return index // 32, (index // 8) % 4, (index // 2) % 4, index % 2
+
+
+def route(ranks, target_of, brick_of, block_of, home_of, slots, block_rows):
+    here = torus(lax.axis_index("dom"))
     same = iota((128, 512), 0) == brick_of[...]
     member = onehot(same)
     earlier = onehot(iota((512, 512), 0) < iota((512, 512), 1))
     ordinal = jnp.sum(jnp.where(same, dot(member, earlier), 0.0), axis=0, keepdims=True)
     homes = jnp.broadcast_to(home_of[...].astype(F32), (8, 128)).astype(BF)
-    home = dot(homes, member)[0:1]
+    there = torus(dot(homes, member)[0:1].astype(I32))
+    away = [(there[k] - here[k] + size) % size for k, size in enumerate((4, 4, 4, 2))]
+    offset = ((away[0] * 4 + away[1]) * 4 + away[2]) * 2 + away[3]
+    rank = dot(ranks[...], onehot(iota((128, 512), 0) == offset))[0:1]
     row = iota((8, 512), 0)
-    pair = jnp.where(row == 0, home, jnp.where(row == 1, ordinal, 0.0)).astype(BF)
+    pair = jnp.where(row == 0, rank, jnp.where(row == 1, ordinal, 0.0)).astype(BF)
     for o in range(2):
         chosen = onehot(iota((512, 512), 0) == target_of[o : o + 1, :])
         picked = dot(pair, chosen)
         slots[o : o + 1, :] = (picked[0:1] * SLOTS + picked[1:2]).astype(I32)
-    to_home = onehot(iota((128, 512), 0) == home.astype(I32))
-    lane = ordinal.astype(I32) + SLOTS * lax.rem(me, 8)
-    at_lane = iota((128, 512), 0) == lane
+    rank = rank.astype(I32)
+    to_rank = onehot(iota((128, 512), 0) == rank)
+    at_lane = iota((128, 512), 0) == ordinal.astype(I32) + SLOTS * (rank % 8)
     block = block_of[...]
     upper = jnp.where(at_lane, (block // 16).astype(F32), 0.0).astype(BF)
     lower = jnp.where(at_lane, (block % 16).astype(F32), 0.0).astype(BF)
-    block_rows[...] = dot_nt(to_home, upper) * 16.0 + dot_nt(to_home, lower)
+    block_rows[...] = dot_nt(to_rank, upper) * 16.0 + dot_nt(to_rank, lower)
 
 
 def middle_eigen(j00, j01, j02, j10, j11, j12, j20, j21, j22):
@@ -146,11 +165,16 @@
 
 
 def stitch_z(first, last):
-    span = iota((8, CROSS), 1) % EZN
-    before = jnp.where(span == 0, pltpu.roll(last, CROSS + 1 - EZN, 1), pltpu.roll(last, 1, 1))
-    after = jnp.where(
-        span == EZN - 1, pltpu.roll(first, EZN - 1, 1), pltpu.roll(first, CROSS - 1, 1)
-    )
+    lane = iota((8, CROSS), 1)
+    span = lane % EZN
+    row = lane - span
+
+    def picked(values, step):
+        at = row + (span + step) % EZN
+        return jnp.take_along_axis(values, at, axis=1, mode="promise_in_bounds")
+
+    before = picked(last, EZN - 1)
+    after = picked(first, 1)
     return 0.5 * (first + before), 0.5 * (last + after)
 
 
@@ -185,7 +209,7 @@
             stage_z[pl.ds(pl.multiple_of(w * 64 + i * 8, 8), 8), :] = total
         return carry
 
-    lax.fori_loop(0, 8, along_z, 0)
+    lax.fori_loop(0, 8, along_z, 0, unroll=8)
     for w in range(4):
         points = [stage_z[pl.ds(w * 64 + j, 8, stride=8), :] for j in range(8)]
         for v in range(4):
@@ -199,18 +223,22 @@
         )
         for i in range(8)
     ]
-    at = pl.ds(pl.multiple_of(o * 512 + layer * CROSS, CROSS), CROSS)
+    totals = []
     for u in range(8):
         total = points[0] * res_x[o, u, 0:1, lanes]
         for i in range(1, 8):
             total = total + points[i] * res_x[o, u, i : i + 1, lanes]
-        upper = total.astype(BF)
-        rows[16 * u : 16 * u + 16, at] = upper
-        rows[128 + 16 * u : 144 + 16 * u, at] = (total - upper.astype(F32)).astype(BF)
-
-
-def differentiate(vel, op_x, op_yz, inv, grad, rims):
+        totals.append(total)
+    piece = jnp.concatenate(totals, axis=0).T
+    upper = piece.astype(BF)
+    at = pl.ds(pl.multiple_of(o * 512 + layer * CROSS, CROSS), CROSS)
+    rows[at, 0:128] = upper
+    rows[at, 128:256] = (piece - upper.astype(F32)).astype(BF)
+
+
+def differentiate(vel, op_x, op_yz, inv, grad, rims, vel_loads):
     for c in range(3):
+        vel_loads[c].wait()
         along_x = dot(op_x[...], vel[c])
         halves = [dot(op_yz[...], vel[c, 256 * half : 256 * half + 256, :]) for half in range(2)]
         for a in range(3):
@@ -243,34 +271,36 @@
 
 
 def kernel(
-    vel_h, inv_h, op_x_h, op_yz_h, target_h, brick_h, block_h, home_h, x_h, y_h, z_h,
+    inv_h, op_x_h, op_yz_h, ranks_h, target_h, brick_h, block_h, home_h, x_h, y_h, z_h, vel_h,
     bricks,
-    vel, inv, op_x, op_yz, target_of, brick_of, block_of, home_of, res_x, res_y, res_z,
-    rims, halo, grad, lam, stage_z, stage_y, rows, slots, block_rows, source, landed,
-    load_sems, halo_send, halo_recv, send_sem, recv_sems, own_sem,
+    inv, op_x, op_yz, ranks, target_of, brick_of, block_of, home_of, res_x, res_y, res_z, vel,
+    rims, halo, grad, lam, stage_z, stage_y, rows, slots, block_rows, source, landed, landed_blocks, places,
+    load_sems, vel_sems, halo_send, halo_recv, send_sem, recv_sems, block_send, block_recv, own_sem,
 ):
     me = lax.axis_index("dom")
     count = lax.axis_size("dom")
-    mine = me // 16
     mesh_id = pl.DeviceIdType.MESH
-
-    far = (vel_h, inv_h, op_x_h, op_yz_h, target_h, brick_h, block_h, home_h, x_h, y_h, z_h)
-    near = (vel, inv, op_x, op_yz, target_of, brick_of, block_of, home_of, res_x, res_y, res_z)
+    y, x, z, core = torus(me)
+    parts = (
+        [lax.rem(y + k, 4) * 32 for k in range(4)],
+        [lax.rem(x + k, 4) * 8 for k in range(4)],
+        [lax.rem(z + k, 4) * 2 for k in range(4)],
+        [lax.rem(core + k, 2) for k in range(2)],
+    )
+    peers = [sum(part[k] for part, k in zip(parts, offset)) for offset in OFFSETS[:-1]]
+
+    far = (inv_h, op_x_h, op_yz_h, ranks_h, target_h, brick_h, block_h, home_h, x_h, y_h, z_h)
+    near = (inv, op_x, op_yz, ranks, target_of, brick_of, block_of, home_of, res_x, res_y, res_z)
     loads = [pltpu.make_async_copy(f, n, load_sems.at[k]) for k, (f, n) in enumerate(zip(far, near))]
-    for load in loads:
+    vel_loads = [pltpu.make_async_copy(vel_h.at[c], vel.at[c], vel_sems.at[c]) for c in range(3)]
+    for load in loads[:2] + vel_loads[:1] + loads[2:3] + vel_loads[1:] + loads[3:]:
         load.start()
     barrier = pltpu.get_barrier_semaphore()
-
-    def greet(step, carry):
-        pl.semaphore_signal(
-            barrier, inc=1, device_id=(lax.rem(me + step, count),), device_id_type=mesh_id
-        )
-        return carry
-
-    lax.fori_loop(1, count, greet, 0)
-    for load in loads[:4]:
+    for peer in peers:
+        pl.semaphore_signal(barrier, inc=1, device_id=(peer,), device_id_type=mesh_id)
+    for load in loads[:3]:
         load.wait()
-    differentiate(vel, op_x, op_yz, inv, grad, rims)
+    differentiate(vel, op_x, op_yz, inv, grad, rims, vel_loads)
 
     def plane_z(t, carry):
         stitch_plane_z(grad, t // 8, pl.multiple_of(lax.rem(t, 8) * 64, 64))
@@ -280,10 +310,10 @@
         eigen_plane(grad, lam, t // 8, pl.multiple_of(lax.rem(t, 8) * 64, 64))
         return carry
 
-    lax.fori_loop(1, 31, plane_z, 0)
-    for load in loads[4:8]:
+    lax.fori_loop(1, 31, plane_z, 0, unroll=2)
+    for load in loads[3:8]:
         load.wait()
-    route(target_of, brick_of, block_of, home_of, slots, block_rows)
+    route(ranks, target_of, brick_of, block_of, home_of, slots, block_rows)
 
     pl.semaphore_wait(barrier, count - 1)
     sends = [
@@ -296,8 +326,14 @@
     ]
     for send in sends:
         send.start()
-
-    lax.fori_loop(1, 31, plane_eigen, 0)
+    for rank, peer in enumerate(peers):
+        pltpu.make_async_remote_copy(
+            src_ref=block_rows.at[pl.ds(rank, 1)], dst_ref=landed_blocks.at[pl.ds(rank, 1)],
+            send_sem=block_send, recv_sem=block_recv,
+            device_id=(peer,), device_id_type=mesh_id,
+        ).start()
+
+    lax.fori_loop(1, 31, plane_eigen, 0, unroll=2)
     for load in loads[8:]:
         load.wait()
 
@@ -324,76 +360,70 @@
 
     slot_row = jnp.concatenate([slots[0:1, :], slots[1:2, :]], axis=1)
 
-    def push(chunk, first):
-        def one(step, carry):
-            peer = chunk * 16 + lax.rem(me + step, 16)
+    def push(chunk):
+        for rank in range(16 * chunk, min(16 * chunk + 16, 127)):
             pltpu.make_async_remote_copy(
-                src_ref=source.at[peer], dst_ref=landed.at[me],
-                send_sem=send_sem, recv_sem=recv_sems.at[mine],
-                device_id=(peer,), device_id_type=mesh_id,
+                src_ref=source.at[rank], dst_ref=landed.at[rank],
+                send_sem=send_sem, recv_sem=recv_sems.at[chunk],
+                device_id=(peers[rank],), device_id_type=mesh_id,
             ).start()
-            return carry
-
-        lax.fori_loop(first, 16, one, 0)
-
-    def pack(g, carry):
-        chunk = lax.rem(mine + 1 + g, 8)
-        base = pl.multiple_of(chunk * 16, 16)
-        chosen = onehot(iota((256, 1024), 0) + chunk * 256 == slot_row)
-        packed = dot_nt(chosen, rows[...])
-        source[pl.ds(base, 16), 0:SLOTS, :] = (packed[:, 0:128] + packed[:, 128:256]).reshape(16, SLOTS, 128)
-        source[pl.ds(base, 16), SLOTS, :] = block_rows[pl.ds(base, 16), :]
-
-        @pl.when(g > 0)
-        def _():
-            push(lax.rem(mine + g, 8), 0)
-
-        return carry
-
-    lax.fori_loop(0, 8, pack, 0)
+
+    pushed = 0
+    for chunk, chunks in PACKS:
+        at = slice(16 * chunk, 16 * chunk + 16 * chunks)
+        chosen = onehot(iota((256 * chunks, 1024), 0) + chunk * 256 == slot_row)
+        packed = dot(chosen, rows[...])
+        source[at] = (packed[:, 0:128] + packed[:, 128:256]).reshape(16 * chunks, SLOTS, 128)
+        while pushed < chunk:
+            push(pushed)
+            pushed += 1
     for send in sends:
         send.wait_send()
-    push(mine, 1)
-    own = pltpu.make_async_copy(source.at[me], landed.at[me], own_sem)
+    while pushed < 8:
+        push(pushed)
+        pushed += 1
+    own = pltpu.make_async_copy(source.at[127], landed.at[127], own_sem)
     own.start()
     own.wait()
 
-    def arrived(chunk, number):
-        part = landed.at[pl.ds(0, number)]
-        pltpu.make_async_remote_copy(
-            src_ref=part, dst_ref=part, send_sem=send_sem, recv_sem=recv_sems.at[chunk],
+    def drained(ref, send, recv):
+        return pltpu.make_async_remote_copy(
+            src_ref=ref, dst_ref=ref, send_sem=send, recv_sem=recv,
             device_id=(me,), device_id_type=mesh_id,
-        ).wait_recv()
-
-    def unpack(chunk):
-        base = pl.multiple_of(chunk * 16, 16)
-        block = jnp.sum(landed[pl.ds(base, 16), SLOTS, :].reshape(2, 8, 128), axis=1).astype(I32)
-        named = jnp.concatenate([block[0:1], block[1:2]], axis=1)
-        values = landed[pl.ds(base, 16), 0:SLOTS, :].reshape(256, 128)
+        )
+
+    blocks_in = drained(landed_blocks.at[pl.ds(0, count - 1)], block_send, block_recv)
+    blocks_in.wait_recv()
+    blocks_in.wait_send()
+    landed_blocks[127:128, :] = block_rows[127:128, :]
+    named = jnp.sum(landed_blocks[...].reshape(16, 8, 128), axis=1).astype(I32)
+
+    def place(step, carry):
+        base = pl.multiple_of(step * 256, 256)
+        row = iota((256, 128), 0) + base
+        for n in range(16):
+            places[pl.ds(base, 256), 128 * n : 128 * n + 128] = onehot(row == named[n : n + 1, :])
+        return carry
+
+    lax.fori_loop(0, 8, place, 0)
+
+    def unpack(chunk, chunks):
+        for n in range(chunk, chunk + chunks):
+            part = landed.at[pl.ds(16 * n, 15 if n == 7 else 16)]
+            drained(part, send_sem, recv_sems.at[n]).wait_recv()
+        values = landed[16 * chunk : 16 * chunk + 16 * chunks].reshape(256 * chunks, 128)
         upper = values.astype(BF)
         lower = (values - upper.astype(F32)).astype(BF)
         both = jnp.concatenate([upper, lower], axis=1)
-        for part in range(8):
-            term = dot(onehot(iota((256, 256), 0) + 256 * part == named), both)
-            at = slice(256 * part, 256 * part + 256)
-            bricks[0, at, :] += term[:, 0:128] + term[:, 128:256]
-
-    bricks[...] = jnp.zeros_like(bricks)
-
-    def receive(g, carry):
-        chunk = lax.rem(mine + 7 - g, 8)
-        arrived(chunk, 16)
-        unpack(chunk)
-        return carry
-
-    lax.fori_loop(0, 7, receive, 0)
-    arrived(mine, 15)
-    unpack(mine)
-    everything = source.at[pl.ds(0, count - 1)]
-    pltpu.make_async_remote_copy(
-        src_ref=everything, dst_ref=everything, send_sem=send_sem, recv_sem=recv_sems.at[0],
-        device_id=(me,), device_id_type=mesh_id,
-    ).wait_send()
+        for part in range(4):
+            at = slice(512 * part, 512 * part + 512)
+            term = dot(places[at, 256 * chunk : 256 * chunk + 256 * chunks], both)
+            term = term[:, 0:128] + term[:, 128:256]
+            bricks[0, at, :] = term if chunk == 0 else bricks[0, at, :] + term
+
+    for chunk, chunks in GROUPS:
+        unpack(chunk, chunks)
+    drained(source.at[pl.ds(0, count - 1)], send_sem, recv_sems.at[0]).wait_send()
 
 
 def operators():
@@ -407,10 +437,13 @@
 
 def shards(velocity, inverse_sizes, resample_x, resample_y, resample_z, piece_target, target_brick, target_block, brick_home):
     op_x, op_yz = operators()
+    ranks = np.zeros((8, 128), np.float32)
+    for rank, (y, x, z, core) in enumerate(OFFSETS):
+        ranks[:, ((y * 4 + x) * 4 + z) * 2 + core] = rank
     operands = (
-        velocity, inverse_sizes, op_x, op_yz,
+        inverse_sizes, op_x, op_yz, jnp.asarray(ranks).astype(BF),
         piece_target, target_brick.reshape(1, 512), target_block.reshape(1, 512), brick_home.reshape(1, 128),
-        resample_x, resample_y, resample_z,
+        resample_x, resample_y, resample_z, velocity,
     )
     scratch = [pltpu.VMEM(array.shape, array.dtype) for array in operands]
     scratch += [
@@ -420,16 +453,21 @@
         pltpu.VMEM((LAYERS, 512, 128), F32),
         pltpu.VMEM((256, 128), F32),
         pltpu.VMEM((128, 128), F32),
-        pltpu.VMEM((256, 1024), BF),
+        pltpu.VMEM((1024, 256), BF),
         pltpu.VMEM((2, 512), I32),
         pltpu.VMEM((128, 128), F32),
-        pltpu.VMEM((128, SLOTS + 1, 128), F32),
-        pltpu.VMEM((128, SLOTS + 1, 128), F32),
-        pltpu.SemaphoreType.DMA((len(operands),)),
+        pltpu.VMEM((128, SLOTS, 128), F32),
+        pltpu.VMEM((128, SLOTS, 128), F32),
+        pltpu.VMEM((128, 128), F32),
+        pltpu.VMEM((BLOCKS, BLOCKS), BF),
+        pltpu.SemaphoreType.DMA((len(operands) - 1,)),
+        pltpu.SemaphoreType.DMA((3,)),
         pltpu.SemaphoreType.DMA((2,)),
         pltpu.SemaphoreType.DMA((2,)),
         pltpu.SemaphoreType.DMA,
         pltpu.SemaphoreType.DMA((8,)),
+        pltpu.SemaphoreType.DMA,
+        pltpu.SemaphoreType.DMA,
         pltpu.SemaphoreType.DMA,
     ]
     return pl.pallas_call(
@@ -442,7 +480,7 @@
             collective_id=0, has_side_effects=True, vmem_limit_bytes=VMEM_LIMIT
         ),
         name="step",
-    )(*operands)
+    )(*[pltpu.with_memory_space_constraint(operand, pltpu.HBM) for operand in operands])
 
 
 def solution(mesh):

time: 43.2 us -> 36.9 us (0.85)
  Pallas kernels: 40.8 us -> 35.8 us
  local copies, waits for them, and re-layouts: 2.26 us -> 0.97 us
    pallas_call x1, Pallas kernels: 40.8 us -> 35.8 us  [shards(): pl.pallas_call(kernel, in_specs=[pl.BlockSpec(memory_space=pltpu.HBM)] *...]
    unnamed x1, local copies, waits for them, and re-layouts: 2.26 us -> 0.97 us
where the time goes in v4:
time: 36.9 us; the launch traced here: 36.8 us
  Pallas kernels  35.8 us (97%)
  local copies, waits for them, and re-layouts  0.97 us (3%)
    pallas_call x1, Pallas kernels, shards(): pl.pallas_call(kernel, in_specs=[pl.BlockSpec(memory_space=pltpu.HBM)] *...  35.8 us
    unnamed x1, local copies, waits for them, and re-layouts  0.97 us

profile of v4, /device:TPU:1, one launch (start us, length us, event | category | flops | bytes accessed | tf_op | source)
XLA Modules:
  0.0 36.8 jit_solution(6598170019955379167)
XLA Ops:
  0.0 35.8 %step.1 = f32[1,2048,128]{2,1,0:T(8,128)S(1)} custom-call(f32[3,512]{1,0:T(4,128)} %inv_h.1, bf16[512,512]{1,0:T(8,128)(2,1)} %constant.9.op_x_h, bf16[512,256]{1,0:T(8,128)(2,1)} %constant.10.op_yz_h, bf16[8,128]{1,0:T(8,128)(2,1)} %constant.11.ranks_h, s32[2,512]{1,0:T(2,128)} %target_h.1, s32[1,512]{1,0:T(1,128)} %bitcast.3, s32[1,512]{1,0:T(1,128)} %bitcast.4, ...), custom_call_target="tpu_custom_call" | custom-call | tf_op jit(solution)/shard_map/step/pallas_call | solution.py:473
  35.8 1.0 %copy.14 = f32[1,2048,128]{2,1,0:T(8,128)} copy(f32[1,2048,128]{2,1,0:T(8,128)S(1)} %step.1) | data formatting | bytes 2097152

commit v5 on v4

--- a/solution.py
+++ b/solution.py
@@ -14,6 +14,7 @@
 CROSS = 128
 LAYERS = 4
 SLOTS = 16
+FACE = 392
 BF = jnp.bfloat16
 F32 = jnp.float32
 I32 = jnp.int32
@@ -98,7 +99,7 @@
     return index // 32, (index // 8) % 4, (index // 2) % 4, index % 2
 
 
-def route(ranks, target_of, brick_of, block_of, home_of, slots, block_rows):
+def route(ranks, target_of, brick_of, block_of, home_of, joins, slots, block_rows):
     here = torus(lax.axis_index("dom"))
     same = iota((128, 512), 0) == brick_of[...]
     member = onehot(same)
@@ -109,13 +110,10 @@
     away = [(there[k] - here[k] + size) % size for k, size in enumerate((4, 4, 4, 2))]
     offset = ((away[0] * 4 + away[1]) * 4 + away[2]) * 2 + away[3]
     rank = dot(ranks[...], onehot(iota((128, 512), 0) == offset))[0:1]
-    row = iota((8, 512), 0)
-    pair = jnp.where(row == 0, rank, jnp.where(row == 1, ordinal, 0.0)).astype(BF)
     for o in range(2):
-        chosen = onehot(iota((512, 512), 0) == target_of[o : o + 1, :])
-        picked = dot(pair, chosen)
-        slots[o : o + 1, :] = (picked[0:1] * SLOTS + picked[1:2]).astype(I32)
+        joins[:, 512 * o : 512 * o + 512] = onehot(iota((512, 512), 0) == target_of[o : o + 1, :])
     rank = rank.astype(I32)
+    slots[...] = rank * SLOTS + ordinal.astype(I32)
     to_rank = onehot(iota((128, 512), 0) == rank)
     at_lane = iota((128, 512), 0) == ordinal.astype(I32) + SLOTS * (rank % 8)
     block = block_of[...]
@@ -236,7 +234,7 @@
     rows[at, 128:256] = (piece - upper.astype(F32)).astype(BF)
 
 
-def differentiate(vel, op_x, op_yz, inv, grad, rims, vel_loads):
+def differentiate(vel, op_x, op_yz, inv, grad, rims, faces, vel_loads):
     for c in range(3):
         vel_loads[c].wait()
         along_x = dot(op_x[...], vel[c])
@@ -253,8 +251,17 @@
                     rows = halves[i // 4][at : at + 64, lanes]
                 return rows * inv[a : a + 1, lanes]
 
-            rims[0, m] = block(0, 0)
-            rims[1, m] = block(7, LAYERS - 1)
+            for side, i, layer in ((0, 0, 0), (1, 7, LAYERS - 1)):
+                values = block(i, layer)
+                rims[side, m] = values
+                if a == 0:
+                    lanes = slice(CROSS * layer, CROSS * layer + CROSS)
+                    points = vel[c, 64 * i : 64 * i + 64, lanes]
+                    faces[side, 64 * c : 64 * c + 64, :] = values
+                    faces[side, 192 + 64 * c : 256 + 64 * c, :] = points.astype(F32)
+                    if c == 0:
+                        faces[side, 384:FACE, :] = jnp.zeros((8, CROSS), F32)
+                        faces[side, 384:387, :] = inv[:, lanes]
             for layer in range(LAYERS):
                 for i in range(1, 8):
                     if i == 7 and layer == LAYERS - 1:
@@ -274,7 +281,7 @@
     inv_h, op_x_h, op_yz_h, ranks_h, target_h, brick_h, block_h, home_h, x_h, y_h, z_h, vel_h,
     bricks,
     inv, op_x, op_yz, ranks, target_of, brick_of, block_of, home_of, res_x, res_y, res_z, vel,
-    rims, halo, grad, lam, stage_z, stage_y, rows, slots, block_rows, source, landed, landed_blocks, places,
+    rims, faces, halo, grad, lam, stage_z, stage_y, rows, joins, slots, sums, block_rows, source, landed, landed_blocks, places,
     load_sems, vel_sems, halo_send, halo_recv, send_sem, recv_sems, block_send, block_recv, own_sem,
 ):
     me = lax.axis_index("dom")
@@ -300,7 +307,7 @@
         pl.semaphore_signal(barrier, inc=1, device_id=(peer,), device_id_type=mesh_id)
     for load in loads[:3]:
         load.wait()
-    differentiate(vel, op_x, op_yz, inv, grad, rims, vel_loads)
+    differentiate(vel, op_x, op_yz, inv, grad, rims, faces, vel_loads)
 
     def plane_z(t, carry):
         stitch_plane_z(grad, t // 8, pl.multiple_of(lax.rem(t, 8) * 64, 64))
@@ -311,14 +318,10 @@
         return carry
 
     lax.fori_loop(1, 31, plane_z, 0, unroll=2)
-    for load in loads[3:8]:
-        load.wait()
-    route(ranks, target_of, brick_of, block_of, home_of, slots, block_rows)
-
     pl.semaphore_wait(barrier, count - 1)
     sends = [
         pltpu.make_async_remote_copy(
-            src_ref=rims.at[side], dst_ref=halo.at[1 - side],
+            src_ref=faces.at[side], dst_ref=halo.at[1 - side],
             send_sem=halo_send.at[side], recv_sem=halo_recv.at[1 - side],
             device_id=(lax.rem(me + step, count),), device_id_type=mesh_id,
         )
@@ -326,6 +329,11 @@
     ]
     for send in sends:
         send.start()
+    lax.fori_loop(1, 31, plane_eigen, 0, unroll=5)
+    for load in loads[3:8]:
+        load.wait()
+    route(ranks, target_of, brick_of, block_of, home_of, joins, slots, block_rows)
+
     for rank, peer in enumerate(peers):
         pltpu.make_async_remote_copy(
             src_ref=block_rows.at[pl.ds(rank, 1)], dst_ref=landed_blocks.at[pl.ds(rank, 1)],
@@ -333,7 +341,6 @@
             device_id=(peer,), device_id_type=mesh_id,
         ).start()
 
-    lax.fori_loop(1, 31, plane_eigen, 0, unroll=2)
     for load in loads[8:]:
         load.wait()
 
@@ -349,8 +356,19 @@
     for send in sends:
         send.wait_recv()
     for side, layer, base in ((0, 0, 0), (1, LAYERS - 1, 448)):
-        for m in range(9):
-            grad[layer, m, base : base + 64, :] = 0.5 * (rims[side, m] + halo[side, m])
+        points = jnp.concatenate([halo[side, 192 + 64 * c : 256 + 64 * c, :] for c in range(3)], axis=1)
+        along_face = dot(
+            jnp.concatenate([op_yz[0:64, 0:64], op_yz[256:320, 0:64]], axis=0), points.astype(BF)
+        )
+        for c in range(3):
+            for a in range(3):
+                m = 3 * c + a
+                if a == 0:
+                    other = halo[side, 64 * c : 64 * c + 64, :]
+                else:
+                    other = along_face[64 * a - 64 : 64 * a, CROSS * c : CROSS * c + CROSS]
+                    other = other * halo[side, 384 + a : 385 + a, :]
+                grad[layer, m, base : base + 64, :] = 0.5 * (rims[side, m] + other)
         stitch_plane(grad, layer, slice(base, base + 8), slice(base + 56, base + 64), stitch_y)
     for layer, base in ((0, 0), (LAYERS - 1, 448)):
         stitch_plane_z(grad, layer, base)
@@ -358,7 +376,13 @@
         eigen_plane(grad, lam, layer, base)
     lax.fori_loop(0, 2, resample_of(lambda n: n * (LAYERS - 1)), 0)
 
-    slot_row = jnp.concatenate([slots[0:1, :], slots[1:2, :]], axis=1)
+    for part in range(2):
+        at = slice(256 * part, 256 * part + 256)
+        total = dot(joins[at, :], rows[...])
+        total = total[:, 0:128] + total[:, 128:256]
+        upper = total.astype(BF)
+        sums[at, 0:128] = upper
+        sums[at, 128:256] = (total - upper.astype(F32)).astype(BF)
 
     def push(chunk):
         for rank in range(16 * chunk, min(16 * chunk + 16, 127)):
@@ -371,8 +395,8 @@
     pushed = 0
     for chunk, chunks in PACKS:
         at = slice(16 * chunk, 16 * chunk + 16 * chunks)
-        chosen = onehot(iota((256 * chunks, 1024), 0) + chunk * 256 == slot_row)
-        packed = dot(chosen, rows[...])
+        chosen = onehot(iota((256 * chunks, 512), 0) + chunk * 256 == slots[...])
+        packed = dot(chosen, sums[...])
         source[at] = (packed[:, 0:128] + packed[:, 128:256]).reshape(16 * chunks, SLOTS, 128)
         while pushed < chunk:
             push(pushed)
@@ -448,13 +472,16 @@
     scratch = [pltpu.VMEM(array.shape, array.dtype) for array in operands]
     scratch += [
         pltpu.VMEM((2, 9, 64, 128), F32),
-        pltpu.VMEM((2, 9, 64, 128), F32),
+        pltpu.VMEM((2, FACE, 128), F32),
+        pltpu.VMEM((2, FACE, 128), F32),
         pltpu.VMEM((LAYERS, 9, 512, 128), F32),
         pltpu.VMEM((LAYERS, 512, 128), F32),
         pltpu.VMEM((256, 128), F32),
         pltpu.VMEM((128, 128), F32),
         pltpu.VMEM((1024, 256), BF),
-        pltpu.VMEM((2, 512), I32),
+        pltpu.VMEM((512, 1024), BF),
+        pltpu.VMEM((1, 512), I32),
+        pltpu.VMEM((512, 256), BF),
         pltpu.VMEM((128, 128), F32),
         pltpu.VMEM((128, SLOTS, 128), F32),
         pltpu.VMEM((128, SLOTS, 128), F32),

time: 36.9 us -> 36.2 us (0.981)
  Pallas kernels: 35.8 us -> 35.1 us
    pallas_call x1, Pallas kernels: 35.8 us -> 35.1 us  [shards(): pl.pallas_call(kernel, in_specs=[pl.BlockSpec(memory_space=pltpu.HBM)] *...]
where the time goes in v5:
time: 36.2 us; the launch traced here: 36.1 us
  Pallas kernels  35.1 us (97%)
  local copies, waits for them, and re-layouts  0.97 us (3%)
    pallas_call x1, Pallas kernels, shards(): pl.pallas_call(kernel, in_specs=[pl.BlockSpec(memory_space=pltpu.HBM)] *...  35.1 us
    unnamed x1, local copies, waits for them, and re-layouts  0.97 us

profile of v5, /device:TPU:1, one launch (start us, length us, event | category | flops | bytes accessed | tf_op | source)
XLA Modules:
  0.0 36.1 jit_solution(4259093427476080706)
XLA Ops:
  0.0 35.1 %step.1 = f32[1,2048,128]{2,1,0:T(8,128)S(1)} custom-call(f32[3,512]{1,0:T(4,128)} %inv_h.1, bf16[512,512]{1,0:T(8,128)(2,1)} %constant.9.op_x_h, bf16[512,256]{1,0:T(8,128)(2,1)} %constant.10.op_yz_h, bf16[8,128]{1,0:T(8,128)(2,1)} %constant.11.ranks_h, s32[2,512]{1,0:T(2,128)} %target_h.1, s32[1,512]{1,0:T(1,128)} %bitcast.3, s32[1,512]{1,0:T(1,128)} %bitcast.4, ...), custom_call_target="tpu_custom_call" | custom-call | tf_op jit(solution)/shard_map/step/pallas_call | solution.py:500
  35.1 1.0 %copy.14 = f32[1,2048,128]{2,1,0:T(8,128)} copy(f32[1,2048,128]{2,1,0:T(8,128)S(1)} %step.1) | data formatting | bytes 2097152

commit v6 on v5

--- a/solution.py
+++ b/solution.py
@@ -194,22 +194,24 @@
         lam[layer, at, :] = middle_eigen(*[grad[layer, m, at, :] for m in range(9)])
 
 
-def resample(layer, o, lam, res_x, res_y, res_z, rows, stage_z, stage_y):
+def resample_along_z(layer, lam, res_z, stage_z):
     lanes = pl.ds(pl.multiple_of(layer * CROSS, CROSS), CROSS)
-
-    def along_z(i, carry):
-        base = i * 64
-        points = [lam[layer, pl.ds(base + k, 8, stride=8), :] for k in range(8)]
-        for w in range(4):
-            total = points[0] * res_z[o, w, 0:1, lanes]
-            for k in range(1, 8):
-                total = total + points[k] * res_z[o, w, k : k + 1, lanes]
-            stage_z[pl.ds(pl.multiple_of(w * 64 + i * 8, 8), 8), :] = total
-        return carry
-
-    lax.fori_loop(0, 8, along_z, 0, unroll=8)
+    for i in range(8):
+        points = [lam[layer, pl.ds(64 * i + k, 8, stride=8), :] for k in range(8)]
+        for o in range(2):
+            for w in range(4):
+                total = points[0] * res_z[o, w, 0:1, lanes]
+                for k in range(1, 8):
+                    total = total + points[k] * res_z[o, w, k : k + 1, lanes]
+                at = 256 * o + 64 * w + 8 * i
+                stage_z[at : at + 8, :] = total
+
+
+def resample(layer, o, res_x, res_y, rows, stage_z, stage_y):
+    lanes = pl.ds(pl.multiple_of(layer * CROSS, CROSS), CROSS)
+
     for w in range(4):
-        points = [stage_z[pl.ds(w * 64 + j, 8, stride=8), :] for j in range(8)]
+        points = [stage_z[pl.ds(256 * o + 64 * w + j, 8, stride=8), :] for j in range(8)]
         for v in range(4):
             total = points[0] * res_y[o, v, 0:1, lanes]
             for j in range(1, 8):
@@ -317,7 +319,7 @@
         eigen_plane(grad, lam, t // 8, pl.multiple_of(lax.rem(t, 8) * 64, 64))
         return carry
 
-    lax.fori_loop(1, 31, plane_z, 0, unroll=2)
+    lax.fori_loop(1, 31, plane_z, 0, unroll=5)
     pl.semaphore_wait(barrier, count - 1)
     sends = [
         pltpu.make_async_remote_copy(
@@ -346,8 +348,9 @@
 
     def resample_of(layer_of):
         def both(n, carry):
+            resample_along_z(layer_of(n), lam, res_z, stage_z)
             for o in range(2):
-                resample(layer_of(n), o, lam, res_x, res_y, res_z, rows, stage_z, stage_y)
+                resample(layer_of(n), o, res_x, res_y, rows, stage_z, stage_y)
             return carry
 
         return both
@@ -476,7 +479,7 @@
         pltpu.VMEM((2, FACE, 128), F32),
         pltpu.VMEM((LAYERS, 9, 512, 128), F32),
         pltpu.VMEM((LAYERS, 512, 128), F32),
-        pltpu.VMEM((256, 128), F32),
+        pltpu.VMEM((512, 128), F32),
         pltpu.VMEM((128, 128), F32),
         pltpu.VMEM((1024, 256), BF),
         pltpu.VMEM((512, 1024), BF),

time: 36.2 us -> 36.1 us (level)
  no operation moved by 1% of the time
where the time goes in v6:
time: 36.1 us; the launch traced here: 36 us
  Pallas kernels  35 us (97%)
  local copies, waits for them, and re-layouts  0.97 us (3%)
    pallas_call x1, Pallas kernels, shards(): pl.pallas_call(kernel, in_specs=[pl.BlockSpec(memory_space=pltpu.HBM)] *...  35 us
    unnamed x1, local copies, waits for them, and re-layouts  0.97 us

profile of v6, /device:TPU:1, one launch (start us, length us, event | category | flops | bytes accessed | tf_op | source)
XLA Modules:
  0.0 36.0 jit_solution(8176735324664705008)
XLA Ops:
  0.0 35.0 %step.1 = f32[1,2048,128]{2,1,0:T(8,128)S(1)} custom-call(f32[3,512]{1,0:T(4,128)} %inv_h.1, bf16[512,512]{1,0:T(8,128)(2,1)} %constant.9.op_x_h, bf16[512,256]{1,0:T(8,128)(2,1)} %constant.10.op_yz_h, bf16[8,128]{1,0:T(8,128)(2,1)} %constant.11.ranks_h, s32[2,512]{1,0:T(2,128)} %target_h.1, s32[1,512]{1,0:T(1,128)} %bitcast.3, s32[1,512]{1,0:T(1,128)} %bitcast.4, ...), custom_call_target="tpu_custom_call" | custom-call | tf_op jit(solution)/shard_map/step/pallas_call | solution.py:503
  35.0 1.0 %copy.14 = f32[1,2048,128]{2,1,0:T(8,128)} copy(f32[1,2048,128]{2,1,0:T(8,128)S(1)} %step.1) | data formatting | bytes 2097152
